TPU v7x, 256 devices: a whole 4x4x8 slice. The times are simulated.
256 devices in a mesh: blk: 256 (over x, z, y, core).
Axes of the slice: x: 4, y: 4, z: 8, core: 2. Of those that a mesh axis runs over, the one named last changes fastest.
Arguments:
- query_states: bfloat16 [65536, 4096], P('blk'), may hold values from -6 to 6
- rotated_key_state: bfloat16 [65536, 1024], P('blk'), may hold values from -6 to 6
- value_state_rows: bfloat16 [65536, 1024], P('blk'), may hold values from -6 to 6
- positions: int32 [65536], P('blk'), may hold values from 0 to 1535, as said below
- residual: bfloat16 [65536, 4096], P('blk'), may hold values from -6 to 6
- norm_gain: float32 [4096], replicated, may hold values from 0.1 to 1.9
- gate_weight: bfloat16 [14336, 4096], P('blk'), may hold values from -0.09375 to 0.09375
- up_weight: bfloat16 [14336, 4096], P('blk'), may hold values from -0.09375 to 0.09375
- down_weight: bfloat16 [14336, 4096], P('blk'), may hold values from -0.375 to 0.375
Outputs:
- attended: bfloat16 [65536, 4096], P('blk')
- ffn_part: bfloat16 [65536, 4096], P('blk')
Inputs may be any that keep to these rules, and one draw needn't show every extreme that they name: positions[0] is 0 and every later entry is 0 or one more than the entry before it.
All inputs are finite; a program needn't handle non-finite values.
Results may differ from a plain program's by a relative error of at most 0.0065.
Values may be sent and summed in bfloat16 or wider, within the bound.
No kernel may reach another device: no remote copies, remote signals or barrier semaphores. Data moves between devices by JAX's collectives and lax.ppermute only.
A program may use at most 64 MiB of HBM per device.

v0:
```python
import math

import jax
import jax.numpy as jnp
from jax import lax
from jax.sharding import PartitionSpec as P

QUERY_HEADS = 32
KEY_VALUE_HEADS = 8
HEAD_SIZE = 128
WINDOW_BLOCKS = 4
FFN_STEPS = 4


def passed_along(value, axis, by):
    length = lax.axis_size(axis)
    pairs = [(i, i + by) for i in range(length) if 0 <= i + by < length]
    return lax.ppermute(value, axis, pairs)


def shifted(value, axis, steps):
    count = lax.axis_size(axis)
    pairs = [(source, (source + steps) % count) for source in range(count)]
    return lax.ppermute(value, axis, pairs)


def shard_term(rows_in, gate_rows, up_rows, down_rows):
    contract = (((1,), (1,)), ((), ()))
    gate_value = lax.dot_general(rows_in, gate_rows, contract, preferred_element_type=jnp.float32)
    up_value = lax.dot_general(rows_in, up_rows, contract, preferred_element_type=jnp.float32)
    hidden = (jax.nn.silu(gate_value) * up_value).astype(jnp.bfloat16)
    return jnp.dot(hidden, down_rows, preferred_element_type=jnp.float32)


def per_device(
    query_states,
    rotated_key_state,
    value_state_rows,
    positions,
    residual,
    norm_gain,
    gate_weight,
    up_weight,
    down_weight,
):
    block_rows = query_states.shape[0]
    device_index = lax.axis_index("blk")
    heads_per_group = QUERY_HEADS // KEY_VALUE_HEADS
    arrived = [(rotated_key_state, value_state_rows)]
    current = (rotated_key_state, value_state_rows)
    for offset in range(1, WINDOW_BLOCKS):
        current = passed_along((current[0], current[1]), "blk", 1)
        arrived.append(current)
    ordered = arrived[::-1]
    key_window = jnp.concatenate([block_pair[0] for block_pair in ordered], axis=0)
    value_window = jnp.concatenate([block_pair[1] for block_pair in ordered], axis=0)
    query_index = device_index * block_rows + jnp.arange(block_rows, dtype=jnp.int32)
    key_index = (device_index - (WINDOW_BLOCKS - 1)) * block_rows + jnp.arange(
        WINDOW_BLOCKS * block_rows, dtype=jnp.int32
    )
    visible = (key_index[None, :] <= query_index[:, None]) & (
        key_index[None, :] >= (query_index - positions)[:, None]
    )
    score_scale = 1.0 / math.sqrt(HEAD_SIZE)

    def group_of_head(group_index, attended_rows):
        query_block = lax.dynamic_slice_in_dim(
            query_states, group_index * heads_per_group * HEAD_SIZE, heads_per_group * HEAD_SIZE, 1
        )
        query_block = query_block.reshape(block_rows, heads_per_group, HEAD_SIZE)
        key_block = lax.dynamic_slice_in_dim(key_window, group_index * HEAD_SIZE, HEAD_SIZE, 1)
        value_block = lax.dynamic_slice_in_dim(value_window, group_index * HEAD_SIZE, HEAD_SIZE, 1)
        scores = (
            jnp.einsum("trd,kd->rtk", query_block, key_block, preferred_element_type=jnp.float32)
            * score_scale
        )
        scores = jnp.where(visible[None], scores, -jnp.inf)
        row_max = jnp.max(scores, axis=-1, keepdims=True)
        weights = jnp.exp(scores - row_max)
        denominator = jnp.sum(weights, axis=-1, keepdims=True)
        mixed = (
            jnp.einsum(
                "rtk,kd->rtd",
                weights.astype(jnp.bfloat16),
                value_block,
                preferred_element_type=jnp.float32,
            )
            / denominator
        )
        result = (
            jnp.transpose(mixed, (1, 0, 2))
            .reshape(block_rows, heads_per_group * HEAD_SIZE)
            .astype(jnp.bfloat16)
        )
        return lax.dynamic_update_slice_in_dim(
            attended_rows, result, group_index * heads_per_group * HEAD_SIZE, 1
        )

    attended = lax.fori_loop(
        0,
        KEY_VALUE_HEADS,
        group_of_head,
        jnp.zeros((block_rows, QUERY_HEADS * HEAD_SIZE), jnp.bfloat16),
    )
    stream = residual.astype(jnp.float32) + attended.astype(jnp.float32)
    normed = (
        stream * lax.rsqrt(jnp.mean(stream * stream, axis=-1, keepdims=True) + 1e-05) * norm_gain
    ).astype(jnp.bfloat16)
    ffn_total = shard_term(normed, gate_weight, up_weight, down_weight)
    current_weights = (gate_weight, up_weight, down_weight)
    for offset in range(1, FFN_STEPS):
        current_weights = shifted(
            (current_weights[0], current_weights[1], current_weights[2]), "blk", -1
        )
        ffn_total = ffn_total + shard_term(
            normed, current_weights[0], current_weights[1], current_weights[2]
        )
    return (attended, ffn_total.astype(jnp.bfloat16))


def solution(mesh):
    in_specs = (
        P("blk", None),
        P("blk", None),
        P("blk", None),
        P("blk"),
        P("blk", None),
        P(),
        P("blk", None),
        P("blk", None),
        P("blk", None),
    )
    out_specs = (P("blk", None), P("blk", None))
    return jax.shard_map(
        per_device, mesh=mesh, in_specs=in_specs, out_specs=out_specs, check_vma=False
    )
```

profile of v0, /device:TPU:6, one launch (start us, length us, event | category | flops | bytes accessed | tf_op | source)
XLA Modules:
  0.0 155.3 jit_solution(14664626979332316240)
XLA Ops:
  0.6 1.2 copy.18
  1.9 1.9 %collective-permute-start.3 = (bf16[256,1024]{0,1:T(8,128)(2,1)S(1)}, bf16[256,1024]{0,1:T(8,128)(2,1)S(1)}, u32[]{:S(2)}, u32[]{:S(2)}) collective-permute-start(bf16[256,1024]{0,1:T(8,128)(2,1)S(1)} %copy.18), channel_id=1, source_target_pairs={{0,1},{1,2},{2,3},{3,4},{4,5},{5,6},{6,7},{7,8},{8,9},{9,10},{10,1... | collective-permute-start | bytes 1572872 | tf_op jit(solution)/shard_map/ppermute | solution.py:18
  3.8 3.6 %collective-permute-start = (bf16[256,1024]{1,0:T(8,128)(2,1)}, bf16[256,1024]{1,0:T(8,128)(2,1)S(1)}, u32[]{:S(2)}, u32[]{:S(2)}) collective-permute-start(bf16[256,1024]{1,0:T(8,128)(2,1)} %param.12), channel_id=1, source_target_pairs={{0,1},{1,2},{2,3},{3,4},{4,5},{5,6},{6,7},{7,8},{8,9},{9,10},{10,1... | collective-permute-start | bytes 1572872 | tf_op jit(solution)/shard_map/ppermute | solution.py:18
  7.4 11.3 %collective-permute-done.3 = bf16[256,1024]{0,1:T(8,128)(2,1)S(1)} collective-permute-done((bf16[256,1024]{0,1:T(8,128)(2,1)S(1)}, bf16[256,1024]{0,1:T(8,128)(2,1)S(1)}, u32[]{:S(2)}, u32[]{:S(2)}) %collective-permute-start.3) | collective-permute-done | bytes 524320 | tf_op jit(solution)/shard_map/ppermute | solution.py:18
  18.7 1.9 %collective-permute-start.4 = (bf16[256,1024]{0,1:T(8,128)(2,1)S(1)}, bf16[256,1024]{0,1:T(8,128)(2,1)S(1)}, u32[]{:S(2)}, u32[]{:S(2)}) collective-permute-start(bf16[256,1024]{0,1:T(8,128)(2,1)S(1)} %collective-permute-done.3), channel_id=1, source_target_pairs={{0,1},{1,2},{2,3},{3,4},{4,5},{5,6},{6,7},{7,8},{8,9},{9,10},{10,1... | collective-permute-start | bytes 1572872 | tf_op jit(solution)/shard_map/ppermute | solution.py:18
  20.6 6.0 %collective-permute-start.6 = (bf16[56,4096]{1,0:T(8,128)(2,1)}, bf16[56,4096]{1,0:T(8,128)(2,1)}, u32[]{:S(2)}, u32[]{:S(2)}) collective-permute-start(bf16[56,4096]{1,0:T(8,128)(2,1)} %param.17), channel_id=1, source_target_pairs={{0,255},{1,0},{2,1},{3,2},{4,3},{5,4},{6,5},{7,6},{8,7},{9,8},{10,... | collective-permute-start | bytes 1376264 | tf_op jit(solution)/shard_map/ppermute | solution.py:24
  26.8 2.3 %collective-permute-start.1 = (bf16[256,1024]{1,0:T(8,128)(2,1)S(1)}, bf16[256,1024]{1,0:T(8,128)(2,1)S(1)}, u32[]{:S(2)}, u32[]{:S(2)}) collective-permute-start(bf16[256,1024]{1,0:T(8,128)(2,1)S(1)} %collective-permute-done), channel_id=1, source_target_pairs={{0,1},{1,2},{2,3},{3,4},{4,5},{5,6},{6,7},{7,8},{8,9},{9,10},{10,1... | collective-permute-start | bytes 1572872 | tf_op jit(solution)/shard_map/ppermute | solution.py:18
  29.1 4.2 %collective-permute-done.4 = bf16[256,1024]{0,1:T(8,128)(2,1)S(1)} collective-permute-done((bf16[256,1024]{0,1:T(8,128)(2,1)S(1)}, bf16[256,1024]{0,1:T(8,128)(2,1)S(1)}, u32[]{:S(2)}, u32[]{:S(2)}) %collective-permute-start.4) | collective-permute-done | bytes 524320 | tf_op jit(solution)/shard_map/ppermute | solution.py:18
  33.4 1.9 %collective-permute-start.5 = (bf16[256,1024]{0,1:T(8,128)(2,1)S(1)}, bf16[256,1024]{0,1:T(8,128)(2,1)S(1)}, u32[]{:S(2)}, u32[]{:S(2)}) collective-permute-start(bf16[256,1024]{0,1:T(8,128)(2,1)S(1)} %collective-permute-done.4), channel_id=1, source_target_pairs={{0,1},{1,2},{2,3},{3,4},{4,5},{5,6},{6,7},{7,8},{8,9},{9,10},{10,1... | collective-permute-start | bytes 1572872 | tf_op jit(solution)/shard_map/ppermute | solution.py:18
  35.3 6.0 %collective-permute-start.9 = (bf16[56,4096]{1,0:T(8,128)(2,1)}, bf16[56,4096]{1,0:T(8,128)(2,1)}, u32[]{:S(2)}, u32[]{:S(2)}) collective-permute-start(bf16[56,4096]{1,0:T(8,128)(2,1)} %collective-permute-done.6), channel_id=1, source_target_pairs={{0,255},{1,0},{2,1},{3,2},{4,3},{5,4},{6,5},{7,6},{8,7},{9,8},{10,... | collective-permute-start | bytes 1376264 | tf_op jit(solution)/shard_map/ppermute | solution.py:24
  41.3 2.6 %collective-permute-start.10 = (bf16[56,4096]{1,0:T(8,128)(2,1)}, bf16[56,4096]{1,0:T(8,128)(2,1)}, u32[]{:S(2)}, u32[]{:S(2)}) collective-permute-start(bf16[56,4096]{1,0:T(8,128)(2,1)} %collective-permute-done.7), channel_id=1, source_target_pairs={{0,255},{1,0},{2,1},{3,2},{4,3},{5,4},{6,5},{7,6},{8,7},{9,8},{10,... | collective-permute-start | bytes 1376264 | tf_op jit(solution)/shard_map/ppermute | solution.py:24
  44.0 4.9 %collective-permute-start.11 = (bf16[56,4096]{1,0:T(8,128)(2,1)}, bf16[56,4096]{1,0:T(8,128)(2,1)}, u32[]{:S(2)}, u32[]{:S(2)}) collective-permute-start(bf16[56,4096]{1,0:T(8,128)(2,1)} %collective-permute-done.8), channel_id=1, source_target_pairs={{0,255},{1,0},{2,1},{3,2},{4,3},{5,4},{6,5},{7,6},{8,7},{9,8},{10,... | collective-permute-start | bytes 1376264 | tf_op jit(solution)/shard_map/ppermute | solution.py:24
  48.9 4.1 %copy.21 = bf16[256,4096]{0,1:T(8,128)(2,1)} copy(bf16[256,4096]{1,0:T(8,128)(2,1)} %param.15) | data formatting | bytes 4194304 | tf_op args[4]
  53.0 1.9 %collective-permute-start.2 = (bf16[256,1024]{1,0:T(8,128)(2,1)S(1)}, bf16[256,1024]{1,0:T(8,128)(2,1)S(1)}, u32[]{:S(2)}, u32[]{:S(2)}) collective-permute-start(bf16[256,1024]{1,0:T(8,128)(2,1)S(1)} %collective-permute-done.1), channel_id=1, source_target_pairs={{0,1},{1,2},{2,3},{3,4},{4,5},{5,6},{6,7},{7,8},{8,9},{9,10},{10,1... | collective-permute-start | bytes 1572872 | tf_op jit(solution)/shard_map/ppermute | solution.py:18
  55.0 6.0 %collective-permute-start.12 = (bf16[56,4096]{1,0:T(8,128)(2,1)}, bf16[56,4096]{1,0:T(8,128)(2,1)}, u32[]{:S(2)}, u32[]{:S(2)}) collective-permute-start(bf16[56,4096]{1,0:T(8,128)(2,1)} %collective-permute-done.9), channel_id=1, source_target_pairs={{0,255},{1,0},{2,1},{3,2},{4,3},{5,4},{6,5},{7,6},{8,7},{9,8},{10,... | collective-permute-start | bytes 1376264 | tf_op jit(solution)/shard_map/ppermute | solution.py:24
  61.1 2.5 %collective-permute-start.14 = (bf16[56,4096]{1,0:T(8,128)(2,1)}, bf16[56,4096]{1,0:T(8,128)(2,1)}, u32[]{:S(2)}, u32[]{:S(2)}) collective-permute-start(bf16[56,4096]{1,0:T(8,128)(2,1)} %collective-permute-done.11), channel_id=1, source_target_pairs={{0,255},{1,0},{2,1},{3,2},{4,3},{5,4},{6,5},{7,6},{8,7},{9,8},{10,... | collective-permute-start | bytes 1376264 | tf_op jit(solution)/shard_map/ppermute | solution.py:24
  63.6 1.6 %pad_maximum_fusion.1 = bf16[1024,1024]{0,1:T(8,128)(2,1)} fusion(bf16[256,1024]{0,1:T(8,128)(2,1)S(1)} %copy.18, bf16[256,1024]{0,1:T(8,128)(2,1)S(1)} %collective-permute-done.3, bf16[256,1024]{0,1:T(8,128)(2,1)S(1)} %collective-permute-done.4, bf16[256,1024]{0,1:T(8,128)(2,1)S(1)} %collective-permute-done.5), kind=kLoop, calls=%fused_computation.31 | loop fusion | flops 8388608 | bytes 4194304 | tf_op jit(solution)/shard_map/concatenate | solution.py:56
  65.2 2.5 %collective-permute-done.2 = bf16[256,1024]{1,0:T(8,128)(2,1)S(1)} collective-permute-done((bf16[256,1024]{1,0:T(8,128)(2,1)S(1)}, bf16[256,1024]{1,0:T(8,128)(2,1)S(1)}, u32[]{:S(2)}, u32[]{:S(2)}) %collective-permute-start.2) | collective-permute-done | bytes 524320 | tf_op jit(solution)/shard_map/ppermute | solution.py:18
  67.7 1.5 pad_maximum_fusion
  69.3 50.2 %while.16 = (s32[]{:T(128)}, bf16[256,4096]{0,1:T(8,128)(2,1)S(1)}, bf16[1024,1024]{1,0:T(8,128)(2,1)}, bf16[256,4096]{1,0:T(8,128)(2,1)}, bf16[1024,1024]{0,1:T...) while((s32[]{:T(128)}, bf16[256,4096]{0,1:T(8,128)(2,1)S(1)}, ...), condition=%wide.region_3.4_spmd.clone, body=%wide.region_0.3_spmd.clone.sunk | while | flops 549451776 | bytes 16279793 | solution.py:99
  69.3 1.0 constant_dynamic-slice_fusion.2
  70.5 0.3 compare_and_fusion.2
  70.7 1.7 %fusion.83 = (f32[4,256]{1,0:T(4,128)S(1)}, f32[1024,256,4]{1,0,2:T(8,128)S(1)}) fusion(pred[256,1024]{0,1:T(8,128)(4,1)S(1)} %compare_and_fusion.2, bf16[256,4,128]{0,2,1:T(8,128)(2,1)S(1)} %bitcast.73, bf16[1024,1024]{1,0:T(8,128)(2,1)} %get-tuple-element.293, s32[]{:T(128)S(6)} %select_n.59), kind=kOutput, calls=%fused_computation.5.clone.1 | convolution fusion | flops 271580160 | bytes 4984836 | tf_op jit(solution)/shard_map/while/body/eval_jaxpr/trd,kd->rtk/dot_general | solution.py:74
  72.5 0.9 fusion.84
  73.4 2.2 %fusion.85 = bf16[256,4,128]{0,2,1:T(8,128)(2,1)S(1)} fusion(f32[1024,256,4]{1,0,2:T(8,128)S(1)} %get-tuple-element.261, f32[4,256]{1,0:T(4,128)S(1)} %get-tuple-element.262, pred[256,1024]{0,1:T(8,128)(4,1)S(1)} %compare_and_fusion.2, f32[256,4]{0,1:T(4,128)S(1)} %bitcast.75, bf16[1024,1024]{0,1:T(8,128)(2,1)} %get-tuple-element.295, s32[]{:T(128)S(6)} %select_n.59), kind=kOutput, calls=%fused_computation.11.clone.1 | convolution fusion | flops 272891904 | bytes 4988932 | tf_op jit(solution)/shard_map/while/body/eval_jaxpr/rtk,kd->rtd/dot_general | solution.py:82
  75.6 1.0 constant_dynamic-slice_fusion.2
  77.0 1.7 %fusion.83 = (f32[4,256]{1,0:T(4,128)S(1)}, f32[1024,256,4]{1,0,2:T(8,128)S(1)}) fusion(pred[256,1024]{0,1:T(8,128)(4,1)S(1)} %compare_and_fusion.2, bf16[256,4,128]{0,2,1:T(8,128)(2,1)S(1)} %bitcast.73, bf16[1024,1024]{1,0:T(8,128)(2,1)} %get-tuple-element.293, s32[]{:T(128)S(6)} %select_n.59), kind=kOutput, calls=%fused_computation.5.clone.1 | convolution fusion | flops 271580160 | bytes 4984836 | tf_op jit(solution)/shard_map/while/body/eval_jaxpr/trd,kd->rtk/dot_general | solution.py:74
  78.8 0.9 fusion.84
  79.7 2.2 %fusion.85 = bf16[256,4,128]{0,2,1:T(8,128)(2,1)S(1)} fusion(f32[1024,256,4]{1,0,2:T(8,128)S(1)} %get-tuple-element.261, f32[4,256]{1,0:T(4,128)S(1)} %get-tuple-element.262, pred[256,1024]{0,1:T(8,128)(4,1)S(1)} %compare_and_fusion.2, f32[256,4]{0,1:T(4,128)S(1)} %bitcast.75, bf16[1024,1024]{0,1:T(8,128)(2,1)} %get-tuple-element.295, s32[]{:T(128)S(6)} %select_n.59), kind=kOutput, calls=%fused_computation.11.clone.1 | convolution fusion | flops 272891904 | bytes 4988932 | tf_op jit(solution)/shard_map/while/body/eval_jaxpr/rtk,kd->rtd/dot_general | solution.py:82
  81.9 1.0 constant_dynamic-slice_fusion.2
  83.3 1.7 %fusion.83 = (f32[4,256]{1,0:T(4,128)S(1)}, f32[1024,256,4]{1,0,2:T(8,128)S(1)}) fusion(pred[256,1024]{0,1:T(8,128)(4,1)S(1)} %compare_and_fusion.2, bf16[256,4,128]{0,2,1:T(8,128)(2,1)S(1)} %bitcast.73, bf16[1024,1024]{1,0:T(8,128)(2,1)} %get-tuple-element.293, s32[]{:T(128)S(6)} %select_n.59), kind=kOutput, calls=%fused_computation.5.clone.1 | convolution fusion | flops 271580160 | bytes 4984836 | tf_op jit(solution)/shard_map/while/body/eval_jaxpr/trd,kd->rtk/dot_general | solution.py:74
  85.0 0.9 fusion.84
  85.9 2.2 %fusion.85 = bf16[256,4,128]{0,2,1:T(8,128)(2,1)S(1)} fusion(f32[1024,256,4]{1,0,2:T(8,128)S(1)} %get-tuple-element.261, f32[4,256]{1,0:T(4,128)S(1)} %get-tuple-element.262, pred[256,1024]{0,1:T(8,128)(4,1)S(1)} %compare_and_fusion.2, f32[256,4]{0,1:T(4,128)S(1)} %bitcast.75, bf16[1024,1024]{0,1:T(8,128)(2,1)} %get-tuple-element.295, s32[]{:T(128)S(6)} %select_n.59), kind=kOutput, calls=%fused_computation.11.clone.1 | convolution fusion | flops 272891904 | bytes 4988932 | tf_op jit(solution)/shard_map/while/body/eval_jaxpr/rtk,kd->rtd/dot_general | solution.py:82
  88.2 1.0 constant_dynamic-slice_fusion.2
  89.6 1.7 %fusion.83 = (f32[4,256]{1,0:T(4,128)S(1)}, f32[1024,256,4]{1,0,2:T(8,128)S(1)}) fusion(pred[256,1024]{0,1:T(8,128)(4,1)S(1)} %compare_and_fusion.2, bf16[256,4,128]{0,2,1:T(8,128)(2,1)S(1)} %bitcast.73, bf16[1024,1024]{1,0:T(8,128)(2,1)} %get-tuple-element.293, s32[]{:T(128)S(6)} %select_n.59), kind=kOutput, calls=%fused_computation.5.clone.1 | convolution fusion | flops 271580160 | bytes 4984836 | tf_op jit(solution)/shard_map/while/body/eval_jaxpr/trd,kd->rtk/dot_general | solution.py:74
  91.3 0.9 fusion.84
  92.2 2.2 %fusion.85 = bf16[256,4,128]{0,2,1:T(8,128)(2,1)S(1)} fusion(f32[1024,256,4]{1,0,2:T(8,128)S(1)} %get-tuple-element.261, f32[4,256]{1,0:T(4,128)S(1)} %get-tuple-element.262, pred[256,1024]{0,1:T(8,128)(4,1)S(1)} %compare_and_fusion.2, f32[256,4]{0,1:T(4,128)S(1)} %bitcast.75, bf16[1024,1024]{0,1:T(8,128)(2,1)} %get-tuple-element.295, s32[]{:T(128)S(6)} %select_n.59), kind=kOutput, calls=%fused_computation.11.clone.1 | convolution fusion | flops 272891904 | bytes 4988932 | tf_op jit(solution)/shard_map/while/body/eval_jaxpr/rtk,kd->rtd/dot_general | solution.py:82
  94.4 1.0 constant_dynamic-slice_fusion.2
  95.8 1.7 %fusion.83 = (f32[4,256]{1,0:T(4,128)S(1)}, f32[1024,256,4]{1,0,2:T(8,128)S(1)}) fusion(pred[256,1024]{0,1:T(8,128)(4,1)S(1)} %compare_and_fusion.2, bf16[256,4,128]{0,2,1:T(8,128)(2,1)S(1)} %bitcast.73, bf16[1024,1024]{1,0:T(8,128)(2,1)} %get-tuple-element.293, s32[]{:T(128)S(6)} %select_n.59), kind=kOutput, calls=%fused_computation.5.clone.1 | convolution fusion | flops 271580160 | bytes 4984836 | tf_op jit(solution)/shard_map/while/body/eval_jaxpr/trd,kd->rtk/dot_general | solution.py:74
  97.6 0.9 fusion.84
  98.5 2.2 %fusion.85 = bf16[256,4,128]{0,2,1:T(8,128)(2,1)S(1)} fusion(f32[1024,256,4]{1,0,2:T(8,128)S(1)} %get-tuple-element.261, f32[4,256]{1,0:T(4,128)S(1)} %get-tuple-element.262, pred[256,1024]{0,1:T(8,128)(4,1)S(1)} %compare_and_fusion.2, f32[256,4]{0,1:T(4,128)S(1)} %bitcast.75, bf16[1024,1024]{0,1:T(8,128)(2,1)} %get-tuple-element.295, s32[]{:T(128)S(6)} %select_n.59), kind=kOutput, calls=%fused_computation.11.clone.1 | convolution fusion | flops 272891904 | bytes 4988932 | tf_op jit(solution)/shard_map/while/body/eval_jaxpr/rtk,kd->rtd/dot_general | solution.py:82
  100.7 1.0 constant_dynamic-slice_fusion.2
  102.1 1.7 %fusion.83 = (f32[4,256]{1,0:T(4,128)S(1)}, f32[1024,256,4]{1,0,2:T(8,128)S(1)}) fusion(pred[256,1024]{0,1:T(8,128)(4,1)S(1)} %compare_and_fusion.2, bf16[256,4,128]{0,2,1:T(8,128)(2,1)S(1)} %bitcast.73, bf16[1024,1024]{1,0:T(8,128)(2,1)} %get-tuple-element.293, s32[]{:T(128)S(6)} %select_n.59), kind=kOutput, calls=%fused_computation.5.clone.1 | convolution fusion | flops 271580160 | bytes 4984836 | tf_op jit(solution)/shard_map/while/body/eval_jaxpr/trd,kd->rtk/dot_general | solution.py:74
  103.9 0.9 fusion.84
  104.8 2.2 %fusion.85 = bf16[256,4,128]{0,2,1:T(8,128)(2,1)S(1)} fusion(f32[1024,256,4]{1,0,2:T(8,128)S(1)} %get-tuple-element.261, f32[4,256]{1,0:T(4,128)S(1)} %get-tuple-element.262, pred[256,1024]{0,1:T(8,128)(4,1)S(1)} %compare_and_fusion.2, f32[256,4]{0,1:T(4,128)S(1)} %bitcast.75, bf16[1024,1024]{0,1:T(8,128)(2,1)} %get-tuple-element.295, s32[]{:T(128)S(6)} %select_n.59), kind=kOutput, calls=%fused_computation.11.clone.1 | convolution fusion | flops 272891904 | bytes 4988932 | tf_op jit(solution)/shard_map/while/body/eval_jaxpr/rtk,kd->rtd/dot_general | solution.py:82
  107.0 1.0 constant_dynamic-slice_fusion.2
  108.4 1.7 %fusion.83 = (f32[4,256]{1,0:T(4,128)S(1)}, f32[1024,256,4]{1,0,2:T(8,128)S(1)}) fusion(pred[256,1024]{0,1:T(8,128)(4,1)S(1)} %compare_and_fusion.2, bf16[256,4,128]{0,2,1:T(8,128)(2,1)S(1)} %bitcast.73, bf16[1024,1024]{1,0:T(8,128)(2,1)} %get-tuple-element.293, s32[]{:T(128)S(6)} %select_n.59), kind=kOutput, calls=%fused_computation.5.clone.1 | convolution fusion | flops 271580160 | bytes 4984836 | tf_op jit(solution)/shard_map/while/body/eval_jaxpr/trd,kd->rtk/dot_general | solution.py:74
  110.1 0.9 fusion.84
  111.0 2.2 %fusion.85 = bf16[256,4,128]{0,2,1:T(8,128)(2,1)S(1)} fusion(f32[1024,256,4]{1,0,2:T(8,128)S(1)} %get-tuple-element.261, f32[4,256]{1,0:T(4,128)S(1)} %get-tuple-element.262, pred[256,1024]{0,1:T(8,128)(4,1)S(1)} %compare_and_fusion.2, f32[256,4]{0,1:T(4,128)S(1)} %bitcast.75, bf16[1024,1024]{0,1:T(8,128)(2,1)} %get-tuple-element.295, s32[]{:T(128)S(6)} %select_n.59), kind=kOutput, calls=%fused_computation.11.clone.1 | convolution fusion | flops 272891904 | bytes 4988932 | tf_op jit(solution)/shard_map/while/body/eval_jaxpr/rtk,kd->rtd/dot_general | solution.py:82
  113.2 1.0 constant_dynamic-slice_fusion.2
  114.7 1.7 %fusion.83 = (f32[4,256]{1,0:T(4,128)S(1)}, f32[1024,256,4]{1,0,2:T(8,128)S(1)}) fusion(pred[256,1024]{0,1:T(8,128)(4,1)S(1)} %compare_and_fusion.2, bf16[256,4,128]{0,2,1:T(8,128)(2,1)S(1)} %bitcast.73, bf16[1024,1024]{1,0:T(8,128)(2,1)} %get-tuple-element.293, s32[]{:T(128)S(6)} %select_n.59), kind=kOutput, calls=%fused_computation.5.clone.1 | convolution fusion | flops 271580160 | bytes 4984836 | tf_op jit(solution)/shard_map/while/body/eval_jaxpr/trd,kd->rtk/dot_general | solution.py:74
  116.4 0.9 fusion.84
  117.3 2.2 %fusion.85 = bf16[256,4,128]{0,2,1:T(8,128)(2,1)S(1)} fusion(f32[1024,256,4]{1,0,2:T(8,128)S(1)} %get-tuple-element.261, f32[4,256]{1,0:T(4,128)S(1)} %get-tuple-element.262, pred[256,1024]{0,1:T(8,128)(4,1)S(1)} %compare_and_fusion.2, f32[256,4]{0,1:T(4,128)S(1)} %bitcast.75, bf16[1024,1024]{0,1:T(8,128)(2,1)} %get-tuple-element.295, s32[]{:T(128)S(6)} %select_n.59), kind=kOutput, calls=%fused_computation.11.clone.1 | convolution fusion | flops 272891904 | bytes 4988932 | tf_op jit(solution)/shard_map/while/body/eval_jaxpr/rtk,kd->rtd/dot_general | solution.py:82
  119.5 3.1 %multiply_reduce_fusion = f32[256]{0:T(256)S(1)} fusion(bf16[256,4096]{0,1:T(8,128)(2,1)S(1)} %get-tuple-element.188, bf16[256,4096]{0,1:T(8,128)(2,1)} %copy.21), kind=kLoop, calls=%fused_computation.28 | loop fusion | flops 5242624 | bytes 4195328 | tf_op jit(solution)/shard_map/reduce_sum | solution.py:107
  122.7 2.1 %multiply_convert_fusion = bf16[256,4096]{0,1:T(8,128)(2,1)S(1)} fusion(bf16[256,4096]{0,1:T(8,128)(2,1)} %copy-done, bf16[256,4096]{0,1:T(8,128)(2,1)S(1)} %copy-done.1, f32[4096]{0:T(1024)S(1)} %copy-done.6, f32[256]{0:T(256)S(1)} %add_rsqrt_fusion), kind=kLoop, calls=%fused_computation.27 | loop fusion | flops 6291456 | bytes 6308864 | tf_op jit(solution)/shard_map/convert_element_type | solution.py:108
  124.9 0.5 fusion.49
  125.3 1.5 fusion.50
  126.8 1.5 fusion.51
  128.3 4.1 %copy.22 = bf16[256,4096]{1,0:T(8,128)(2,1)} copy(bf16[256,4096]{0,1:T(8,128)(2,1)} %copy-done) | data formatting | bytes 4194304
  132.5 3.6 %fusion.28 = f32[256,4096]{1,0:T(8,128)} fusion(bf16[56,4096]{1,0:T(8,128)(2,1)S(1)} %copy-done.3, bf16[256,4096]{0,1:T(8,128)(2,1)S(1)} %multiply_convert_fusion, bf16[56,4096]{1,0:T(8,128)(2,1)S(1)} %copy-done.4, f32[256,56]{0,1:T(8,128)S(1)} %fusion.49), kind=kOutput, calls=%fused_computation.34 | convolution fusion | flops 234967040 | bytes 7266304 | tf_op jit(solution)/shard_map/dot_general | solution.py:32
  136.1 1.5 fusion.52
  137.6 6.1 %convolution_add_fusion.2 = f32[256,4096]{1,0:T(8,128)} fusion(f32[256,4096]{1,0:T(8,128)} %fusion.28, bf16[56,4096]{1,0:T(8,128)(2,1)} %collective-permute-done.8, f32[256,56]{0,1:T(8,128)S(1)} %fusion.50, bf16[256,4096]{0,1:T(8,128)(2,1)S(1)} %multiply_convert_fusion, bf16[56,4096]{1,0:T(8,128)(2,1)} %collective-permute-done.7), kind=kOutput, calls=%fused_computation.25 | convolution fusion | flops 236015616 | bytes 11460608 | tf_op jit(solution)/shard_map/dot_general | solution.py:32
  143.7 6.1 %convolution_add_fusion.1 = f32[256,4096]{1,0:T(8,128)} fusion(f32[256,4096]{1,0:T(8,128)} %convolution_add_fusion.2, bf16[56,4096]{1,0:T(8,128)(2,1)} %collective-permute-done.11, f32[256,56]{0,1:T(8,128)S(1)} %fusion.51, bf16[256,4096]{0,1:T(8,128)(2,1)S(1)} %multiply_convert_fusion, bf16[56,4096]{1,0:T(8,128)(2,1)} %collective-permute-done.10), kind=kOutput, calls=%fused_computation.24 | convolution fusion | flops 236015616 | bytes 11460608 | tf_op jit(solution)/shard_map/dot_general | solution.py:32
  149.9 5.5 %fusion.26 = bf16[256,4096]{1,0:T(8,128)(2,1)} fusion(f32[256,4096]{1,0:T(8,128)} %convolution_add_fusion.1, bf16[56,4096]{1,0:T(8,128)(2,1)} %collective-permute-done.14, f32[256,56]{0,1:T(8,128)S(1)} %fusion.52, bf16[256,4096]{0,1:T(8,128)(2,1)S(1)} %multiply_convert_fusion, bf16[56,4096]{1,0:T(8,128)(2,1)} %collective-permute-done.13), kind=kOutput, calls=%fused_computation.26 | convolution fusion | flops 237064192 | bytes 9363456 | tf_op jit(solution)/shard_map/dot_general | solution.py:32
  (58 shorter events, 3.7 us)
Async XLA Ops:
  1.9 16.8 %collective-permute-start.3 = (bf16[256,1024]{0,1:T(8,128)(2,1)S(1)}, bf16[256,1024]{0,1:T(8,128)(2,1)S(1)}, u32[]{:S(2)}, u32[]{:S(2)}) collective-permute-start(bf16[256,1024]{0,1:T(8,128)(2,1)S(1)} %copy.18), channel_id=1, source_target_pairs={{0,1},{1,2},{2,3},{3,4},{4,5},{5,6},{6,7},{7,8},{8,9},{9,10},{10,1... | collective-permute-start | bytes 1572872 | tf_op jit(solution)/shard_map/ppermute | solution.py:18
  3.8 23.0 %collective-permute-start = (bf16[256,1024]{1,0:T(8,128)(2,1)}, bf16[256,1024]{1,0:T(8,128)(2,1)S(1)}, u32[]{:S(2)}, u32[]{:S(2)}) collective-permute-start(bf16[256,1024]{1,0:T(8,128)(2,1)} %param.12), channel_id=1, source_target_pairs={{0,1},{1,2},{2,3},{3,4},{4,5},{5,6},{6,7},{7,8},{8,9},{9,10},{10,1... | collective-permute-start | bytes 1572872 | tf_op jit(solution)/shard_map/ppermute | solution.py:18
  18.7 14.7 %collective-permute-start.4 = (bf16[256,1024]{0,1:T(8,128)(2,1)S(1)}, bf16[256,1024]{0,1:T(8,128)(2,1)S(1)}, u32[]{:S(2)}, u32[]{:S(2)}) collective-permute-start(bf16[256,1024]{0,1:T(8,128)(2,1)S(1)} %collective-permute-done.3), channel_id=1, source_target_pairs={{0,1},{1,2},{2,3},{3,4},{4,5},{5,6},{6,7},{7,8},{8,9},{9,10},{10,1... | collective-permute-start | bytes 1572872 | tf_op jit(solution)/shard_map/ppermute | solution.py:18
  20.6 14.7 %collective-permute-start.6 = (bf16[56,4096]{1,0:T(8,128)(2,1)}, bf16[56,4096]{1,0:T(8,128)(2,1)}, u32[]{:S(2)}, u32[]{:S(2)}) collective-permute-start(bf16[56,4096]{1,0:T(8,128)(2,1)} %param.17), channel_id=1, source_target_pairs={{0,255},{1,0},{2,1},{3,2},{4,3},{5,4},{6,5},{7,6},{8,7},{9,8},{10,... | collective-permute-start | bytes 1376264 | tf_op jit(solution)/shard_map/ppermute | solution.py:24
  26.6 14.7 %collective-permute-start.7 = (bf16[56,4096]{1,0:T(8,128)(2,1)}, bf16[56,4096]{1,0:T(8,128)(2,1)}, u32[]{:S(2)}, u32[]{:S(2)}) collective-permute-start(bf16[56,4096]{1,0:T(8,128)(2,1)} %param.18), channel_id=1, source_target_pairs={{0,255},{1,0},{2,1},{3,2},{4,3},{5,4},{6,5},{7,6},{8,7},{9,8},{10,... | collective-permute-start | bytes 1376264 | tf_op jit(solution)/shard_map/ppermute | solution.py:24
  26.7 17.3 %collective-permute-start.8 = (bf16[56,4096]{1,0:T(8,128)(2,1)}, bf16[56,4096]{1,0:T(8,128)(2,1)}, u32[]{:S(2)}, u32[]{:S(2)}) collective-permute-start(bf16[56,4096]{1,0:T(8,128)(2,1)} %param.19), channel_id=1, source_target_pairs={{0,255},{1,0},{2,1},{3,2},{4,3},{5,4},{6,5},{7,6},{8,7},{9,8},{10,... | collective-permute-start | bytes 1376264 | tf_op jit(solution)/shard_map/ppermute | solution.py:24
  26.8 26.2 %collective-permute-start.1 = (bf16[256,1024]{1,0:T(8,128)(2,1)S(1)}, bf16[256,1024]{1,0:T(8,128)(2,1)S(1)}, u32[]{:S(2)}, u32[]{:S(2)}) collective-permute-start(bf16[256,1024]{1,0:T(8,128)(2,1)S(1)} %collective-permute-done), channel_id=1, source_target_pairs={{0,1},{1,2},{2,3},{3,4},{4,5},{5,6},{6,7},{7,8},{8,9},{9,10},{10,1... | collective-permute-start | bytes 1572872 | tf_op jit(solution)/shard_map/ppermute | solution.py:18
  33.4 30.3 %collective-permute-start.5 = (bf16[256,1024]{0,1:T(8,128)(2,1)S(1)}, bf16[256,1024]{0,1:T(8,128)(2,1)S(1)}, u32[]{:S(2)}, u32[]{:S(2)}) collective-permute-start(bf16[256,1024]{0,1:T(8,128)(2,1)S(1)} %collective-permute-done.4), channel_id=1, source_target_pairs={{0,1},{1,2},{2,3},{3,4},{4,5},{5,6},{6,7},{7,8},{8,9},{9,10},{10,1... | collective-permute-start | bytes 1572872 | tf_op jit(solution)/shard_map/ppermute | solution.py:18
  35.3 19.7 %collective-permute-start.9 = (bf16[56,4096]{1,0:T(8,128)(2,1)}, bf16[56,4096]{1,0:T(8,128)(2,1)}, u32[]{:S(2)}, u32[]{:S(2)}) collective-permute-start(bf16[56,4096]{1,0:T(8,128)(2,1)} %collective-permute-done.6), channel_id=1, source_target_pairs={{0,255},{1,0},{2,1},{3,2},{4,3},{5,4},{6,5},{7,6},{8,7},{9,8},{10,... | collective-permute-start | bytes 1376264 | tf_op jit(solution)/shard_map/ppermute | solution.py:24
  41.3 19.7 %collective-permute-start.10 = (bf16[56,4096]{1,0:T(8,128)(2,1)}, bf16[56,4096]{1,0:T(8,128)(2,1)}, u32[]{:S(2)}, u32[]{:S(2)}) collective-permute-start(bf16[56,4096]{1,0:T(8,128)(2,1)} %collective-permute-done.7), channel_id=1, source_target_pairs={{0,255},{1,0},{2,1},{3,2},{4,3},{5,4},{6,5},{7,6},{8,7},{9,8},{10,... | collective-permute-start | bytes 1376264 | tf_op jit(solution)/shard_map/ppermute | solution.py:24
  44.0 17.1 %collective-permute-start.11 = (bf16[56,4096]{1,0:T(8,128)(2,1)}, bf16[56,4096]{1,0:T(8,128)(2,1)}, u32[]{:S(2)}, u32[]{:S(2)}) collective-permute-start(bf16[56,4096]{1,0:T(8,128)(2,1)} %collective-permute-done.8), channel_id=1, source_target_pairs={{0,255},{1,0},{2,1},{3,2},{4,3},{5,4},{6,5},{7,6},{8,7},{9,8},{10,... | collective-permute-start | bytes 1376264 | tf_op jit(solution)/shard_map/ppermute | solution.py:24
  48.9 6.0 %copy-start.7 = (s32[256]{0:T(256)S(1)}, s32[256]{0:T(256)}, u32[]{:S(2)}) copy-start(s32[256]{0:T(256)} %param.14) | copy-start | bytes 3076
  53.0 14.7 %collective-permute-start.2 = (bf16[256,1024]{1,0:T(8,128)(2,1)S(1)}, bf16[256,1024]{1,0:T(8,128)(2,1)S(1)}, u32[]{:S(2)}, u32[]{:S(2)}) collective-permute-start(bf16[256,1024]{1,0:T(8,128)(2,1)S(1)} %collective-permute-done.1), channel_id=1, source_target_pairs={{0,1},{1,2},{2,3},{3,4},{4,5},{5,6},{6,7},{7,8},{8,9},{9,10},{10,1... | collective-permute-start | bytes 1572872 | tf_op jit(solution)/shard_map/ppermute | solution.py:18
  54.9 12.8 %copy-start.2 = (bf16[256,1024]{1,0:T(8,128)(2,1)S(1)}, bf16[256,1024]{1,0:T(8,128)(2,1)}, u32[]{:S(2)}) copy-start(bf16[256,1024]{1,0:T(8,128)(2,1)} %param.12) | copy-start | bytes 1572868
  55.0 81.2 %collective-permute-start.12 = (bf16[56,4096]{1,0:T(8,128)(2,1)}, bf16[56,4096]{1,0:T(8,128)(2,1)}, u32[]{:S(2)}, u32[]{:S(2)}) collective-permute-start(bf16[56,4096]{1,0:T(8,128)(2,1)} %collective-permute-done.9), channel_id=1, source_target_pairs={{0,255},{1,0},{2,1},{3,2},{4,3},{5,4},{6,5},{7,6},{8,7},{9,8},{10,... | collective-permute-start | bytes 1376264 | tf_op jit(solution)/shard_map/ppermute | solution.py:24
  61.0 88.9 %collective-permute-start.13 = (bf16[56,4096]{1,0:T(8,128)(2,1)}, bf16[56,4096]{1,0:T(8,128)(2,1)}, u32[]{:S(2)}, u32[]{:S(2)}) collective-permute-start(bf16[56,4096]{1,0:T(8,128)(2,1)} %collective-permute-done.10), channel_id=1, source_target_pairs={{0,255},{1,0},{2,1},{3,2},{4,3},{5,4},{6,5},{7,6},{8,7},{9,8},{10,... | collective-permute-start | bytes 1376264 | tf_op jit(solution)/shard_map/ppermute | solution.py:24
  61.1 88.8 %collective-permute-start.14 = (bf16[56,4096]{1,0:T(8,128)(2,1)}, bf16[56,4096]{1,0:T(8,128)(2,1)}, u32[]{:S(2)}, u32[]{:S(2)}) collective-permute-start(bf16[56,4096]{1,0:T(8,128)(2,1)} %collective-permute-done.11), channel_id=1, source_target_pairs={{0,255},{1,0},{2,1},{3,2},{4,3},{5,4},{6,5},{7,6},{8,7},{9,8},{10,... | collective-permute-start | bytes 1376264 | tf_op jit(solution)/shard_map/ppermute | solution.py:24
  119.5 3.2 %copy-start = (bf16[256,4096]{0,1:T(8,128)(2,1)}, bf16[256,4096]{0,1:T(8,128)(2,1)S(1)}, u32[]{:S(2)}) copy-start(bf16[256,4096]{0,1:T(8,128)(2,1)S(1)} %get-tuple-element.188) | copy-start | bytes 6291460
  119.5 3.2 %copy-start.1 = (bf16[256,4096]{0,1:T(8,128)(2,1)S(1)}, bf16[256,4096]{0,1:T(8,128)(2,1)}, u32[]{:S(2)}) copy-start(bf16[256,4096]{0,1:T(8,128)(2,1)} %copy.21) | copy-start | bytes 6291460
  119.5 3.2 %copy-start.6 = (f32[4096]{0:T(1024)S(1)}, f32[4096]{0:T(1024)}, u32[]{:S(2)}) copy-start(f32[4096]{0:T(1024)} %param.16) | copy-start | bytes 49156
  122.7 2.1 %copy-start.5 = (bf16[56,4096]{1,0:T(8,128)(2,1)S(1)}, bf16[56,4096]{1,0:T(8,128)(2,1)}, u32[]{:S(2)}) copy-start(bf16[56,4096]{1,0:T(8,128)(2,1)} %param.17) | copy-start | bytes 1376260
  128.3 4.2 %copy-start.3 = (bf16[56,4096]{1,0:T(8,128)(2,1)S(1)}, bf16[56,4096]{1,0:T(8,128)(2,1)}, u32[]{:S(2)}) copy-start(bf16[56,4096]{1,0:T(8,128)(2,1)} %param.19) | copy-start | bytes 1376260
  128.3 4.2 %copy-start.4 = (bf16[56,4096]{1,0:T(8,128)(2,1)S(1)}, bf16[56,4096]{1,0:T(8,128)(2,1)}, u32[]{:S(2)}) copy-start(bf16[56,4096]{1,0:T(8,128)(2,1)} %param.18) | copy-start | bytes 1376260
where the time goes:
time: 157 us; the launch traced here: 155 us
  matrix products  57.5 us (37%)
  starting transfers between devices  42 us (27%)
  local copies, waits for them, and re-layouts  18.7 us (12%)
  waiting for transfers between devices  18 us (11%)
  other arithmetic  17.8 us (11%)
    ppermute x9, starting transfers between devices, shifted(): return lax.ppermute(value, axis, pairs)  28.4 us
    dot_general x4, matrix products, shard_term(): return jnp.dot(hidden, down_rows, preferred_element_type=jnp.float32)  21.3 us
    ppermute x6, waiting for transfers between devices, passed_along(): return lax.ppermute(value, axis, pairs)  18 us
    dot_general x8, matrix products, group_of_head(): jnp.einsum('rtk,kd->rtd', weights.astype(jnp.bfloat16), value_block, pref...  17.3 us
    dot_general x8, matrix products, group_of_head(): jnp.einsum('trd,kd->rtk', query_block, key_block, preferred_element_type=...  13.9 us
    ppermute x6, starting transfers between devices, passed_along(): return lax.ppermute(value, axis, pairs)  13.6 us
    unnamed x19, local copies, waits for them, and re-layouts  9.54 us
    dynamic_slice x16, local copies, waits for them, and re-layouts, group_of_head(): lax.dynamic_slice_in_dim(query_states, group_index * heads_per_group * HE...  8.85 us
  transfers between devices with their start and end apart: 15, of which 3 were waited for; matrix products, arithmetic and copies ran while one was open for 56% of the time, Pallas kernels for 0%

commit v1 on v0

v1 whole, which is shorter than its diff:
```python
import functools
import math

import jax
import jax.numpy as jnp
from jax import lax
from jax.experimental import pallas as pl
from jax.experimental.pallas import tpu as pltpu
from jax.sharding import PartitionSpec as P

QUERY_HEADS = 32
KEY_VALUE_HEADS = 8
HEAD_SIZE = 128
WINDOW_BLOCKS = 4
FFN_STEPS = 4
GROUP = QUERY_HEADS // KEY_VALUE_HEADS
UNSEEN = -1e30
EXPONENT = math.log2(math.e) / math.sqrt(HEAD_SIZE)
LANES = 128
NT = (((1,), (1,)), ((), ()))


def to_next(value):
    count = lax.axis_size("blk")
    return lax.ppermute(value, "blk", [(i, i + 1) for i in range(count - 1)])


def to_previous(value):
    count = lax.axis_size("blk")
    return lax.ppermute(value, "blk", [(i, (i - 1) % count) for i in range(count)])


def after(value, done):
    return lax.optimization_barrier((value, done))[0]


def attend_kernel(back, last, *refs):
    q_ref, k_ref, v_ref, position_ref = refs[:4]
    if back > 0:
        stat_ref, sum_ref = refs[4:6]
    bias_ref = refs[-1]
    out = refs[4 if back == 0 else 6 : -1]
    rows = q_ref.shape[0]
    key = lax.broadcasted_iota(jnp.int32, (rows, rows), 0) - back * rows
    query = lax.broadcasted_iota(jnp.int32, (rows, rows), 1)
    seen = key >= query - position_ref[...]
    if back == 0:
        seen = seen & (key <= query)
    bias_ref[...] = jnp.where(seen, 0.0, UNSEEN)

    def group(index, _):
        group_columns = pl.ds(pl.multiple_of(index * HEAD_SIZE, HEAD_SIZE), HEAD_SIZE)
        keys = k_ref[:, group_columns]
        values = v_ref[:, group_columns].T
        for head in range(GROUP):
            columns = pl.ds(pl.multiple_of((index * GROUP + head) * HEAD_SIZE, HEAD_SIZE), HEAD_SIZE)
            features = slice(head * HEAD_SIZE, (head + 1) * HEAD_SIZE)
            for start in range(0, rows, LANES):
                some = slice(start, start + LANES)
                scores = lax.dot_general(
                    keys, q_ref[some, columns], NT, preferred_element_type=jnp.float32
                )
                scores = scores + bias_ref[:, some]
                top = jnp.max(scores, axis=0, keepdims=True)
                if back > 0:
                    top_before = stat_ref[index, head : head + 1, some]
                    top = jnp.maximum(top, top_before)
                weights = jnp.exp2((scores - top) * EXPONENT)
                total = jnp.sum(weights, axis=0, keepdims=True)
                mixed = jnp.dot(values, weights.astype(jnp.bfloat16), preferred_element_type=jnp.float32)
                if back > 0:
                    shrink = jnp.exp2((top_before - top) * EXPONENT)
                    total = total + stat_ref[index, GROUP + head : GROUP + head + 1, some] * shrink
                    mixed = mixed + sum_ref[index, features, some] * shrink
                if last:
                    out[0][some, columns] = (mixed * (1.0 / total)).T.astype(jnp.bfloat16)
                else:
                    out[0][index, head : head + 1, some] = top
                    out[0][index, GROUP + head : GROUP + head + 1, some] = total
                    out[1][index, features, some] = mixed
        return 0

    lax.fori_loop(0, KEY_VALUE_HEADS, group, 0, unroll=4)


def attend(back, last, queries, keys, values, positions, carry=()):
    rows = queries.shape[0]
    if last:
        out_shape = (jax.ShapeDtypeStruct(queries.shape, jnp.bfloat16),)
    else:
        out_shape = (
            jax.ShapeDtypeStruct((KEY_VALUE_HEADS, 2 * GROUP, rows), jnp.float32),
            jax.ShapeDtypeStruct((KEY_VALUE_HEADS, GROUP * HEAD_SIZE, rows), jnp.float32),
        )
    return pl.pallas_call(
        functools.partial(attend_kernel, back, last),
        out_shape=out_shape,
        scratch_shapes=[pltpu.VMEM((rows, rows), jnp.float32)],
        name=f"attend_{back}",
        compiler_params=pltpu.CompilerParams(vmem_limit_bytes=16 << 20),
        cost_estimate=pl.CostEstimate(
            flops=4 * QUERY_HEADS * rows * rows * HEAD_SIZE,
            transcendentals=QUERY_HEADS * rows * rows,
            bytes_accessed=12 << 20,
        ),
    )(queries, keys, values, positions, *carry)


def normed_kernel(attended_ref, residual_ref, gain_ref, out_ref):
    step = 16

    def some(index, _):
        rows = pl.ds(pl.multiple_of(index * step, step), step)
        stream = residual_ref[rows, :].astype(jnp.float32) + attended_ref[rows, :].astype(jnp.float32)
        mean = jnp.mean(stream * stream, axis=-1, keepdims=True)
        out_ref[rows, :] = (stream * lax.rsqrt(mean + 1e-05) * gain_ref[...]).astype(jnp.bfloat16)
        return 0

    lax.fori_loop(0, out_ref.shape[0] // step, some, 0, unroll=2)


def gate_kernel(shards, slot, *refs):
    normed_ref = refs[0]
    weights = refs[1 : 1 + 2 * shards]
    out_ref, lhs_ref = refs[1 + 2 * shards :]
    units = weights[0].shape[0]
    for index, weight in enumerate(weights):
        lhs_ref[index * slot : index * slot + units, :] = weight[...]
        lhs_ref[index * slot + units : (index + 1) * slot, :] = jnp.zeros((slot - units, lhs_ref.shape[1]), lhs_ref.dtype)
    both = lax.dot_general(lhs_ref[...], normed_ref[...], NT, preferred_element_type=jnp.float32)
    for shard in range(shards):
        gate = both[2 * shard * slot : (2 * shard + 1) * slot]
        up = both[(2 * shard + 1) * slot : (2 * shard + 2) * slot]
        out_ref[shard * slot : (shard + 1) * slot, :] = (jax.nn.silu(gate) * up).astype(jnp.bfloat16)


def down_kernel(slot, *refs):
    early_ref, late_ref = refs[:2]
    downs = refs[2 : 2 + FFN_STEPS]
    out_ref, rhs_ref = refs[2 + FFN_STEPS :]
    units = downs[0].shape[0]
    for index, rows in enumerate(downs):
        rhs_ref[index * slot : index * slot + units, :] = rows[...]
        rhs_ref[index * slot + units : (index + 1) * slot, :] = jnp.zeros((slot - units, rhs_ref.shape[1]), rhs_ref.dtype)
    hidden = jnp.concatenate([early_ref[...], late_ref[...]], axis=0).T
    width = 512
    for start in range(0, out_ref.shape[1], width):
        some = slice(start, start + width)
        out_ref[:, some] = jnp.dot(hidden, rhs_ref[:, some], preferred_element_type=jnp.float32).astype(jnp.bfloat16)


def normed_rows(attended, residual, gain):
    rows, features = attended.shape
    return pl.pallas_call(
        normed_kernel,
        out_shape=jax.ShapeDtypeStruct((rows, features), jnp.bfloat16),
        name="norm",
        compiler_params=pltpu.CompilerParams(vmem_limit_bytes=16 << 20),
        cost_estimate=pl.CostEstimate(flops=6 * rows * features, transcendentals=rows, bytes_accessed=6 << 20),
    )(attended, residual, gain)


def gate_up(normed, *weights):
    rows, features = normed.shape
    shards = len(weights) // 2
    units = weights[0].shape[0]
    slot = -(-units // 16) * 16
    return pl.pallas_call(
        functools.partial(gate_kernel, shards, slot),
        out_shape=jax.ShapeDtypeStruct((shards * slot, rows), jnp.bfloat16),
        scratch_shapes=[pltpu.VMEM((2 * shards * slot, features), jnp.bfloat16)],
        name=f"gate_up_{shards}",
        compiler_params=pltpu.CompilerParams(vmem_limit_bytes=16 << 20),
        cost_estimate=pl.CostEstimate(
            flops=4 * shards * rows * features * units,
            transcendentals=shards * rows * units,
            bytes_accessed=2 * shards * units * features * 2 + rows * features * 2,
        ),
    )(normed, *weights)


def down(early, late, downs):
    units, features = downs[0].shape
    rows = early.shape[1]
    slot = late.shape[0]
    return pl.pallas_call(
        functools.partial(down_kernel, slot),
        out_shape=jax.ShapeDtypeStruct((rows, features), jnp.bfloat16),
        scratch_shapes=[pltpu.VMEM((FFN_STEPS * slot, features), jnp.bfloat16)],
        name="down",
        compiler_params=pltpu.CompilerParams(vmem_limit_bytes=16 << 20),
        cost_estimate=pl.CostEstimate(
            flops=2 * FFN_STEPS * rows * features * units,
            transcendentals=0,
            bytes_accessed=4 << 20,
        ),
    )(early, late, *downs)


def per_device(
    query_states,
    rotated_key_state,
    value_state_rows,
    positions,
    residual,
    norm_gain,
    gate_weight,
    up_weight,
    down_weight,
):
    positions = positions[None, :]
    keys = [rotated_key_state]
    values = [value_state_rows]
    gates, ups, downs = [gate_weight], [up_weight], [down_weight]
    keys.append(to_next(keys[0]))
    values.append(to_next(values[0]))
    gates.append(to_previous(gates[0]))
    ups.append(to_previous(ups[0]))
    downs.append(to_previous(downs[0]))

    carry = attend(0, False, query_states, keys[0], values[0], positions)
    keys.append(to_next(after(keys[1], carry[0])))
    gates.append(to_previous(after(gates[1], carry[0])))
    values.append(to_next(after(values[1], carry[0])))
    ups.append(to_previous(after(ups[1], carry[0])))

    carry = attend(1, False, query_states, keys[1], values[1], positions, carry)
    downs.append(to_previous(after(downs[1], carry[0])))
    keys.append(to_next(after(keys[2], carry[0])))
    gates.append(to_previous(after(gates[2], carry[0])))
    values.append(to_next(after(values[2], carry[0])))

    carry = attend(2, False, query_states, keys[2], values[2], positions, carry)
    ups.append(to_previous(after(ups[2], carry[0])))
    downs.append(to_previous(after(downs[2], carry[0])))

    (attended,) = attend(3, True, query_states, keys[3], values[3], positions, carry)
    normed = normed_rows(attended, residual, norm_gain[None, :])
    early = gate_up(normed, gates[0], ups[0], gates[1], ups[1], gates[2], ups[2])
    late = gate_up(normed, gates[3], ups[3])
    ffn_part = down(early, late, downs)
    return (attended, ffn_part)


def solution(mesh):
    rows = P("blk", None)
    in_specs = (rows, rows, rows, P("blk"), rows, P(), rows, rows, rows)
    return jax.shard_map(
        per_device, mesh=mesh, in_specs=in_specs, out_specs=(rows, rows), check_vma=False
    )
```

time: 157 us -> 72.8 us (0.46)
  matrix products: 57.5 us -> 0 us
  Pallas kernels: 0 us -> 24.2 us
  other arithmetic: 17.8 us -> 0 us
  local copies, waits for them, and re-layouts: 18.7 us -> 6.22 us
  waiting for transfers between devices: 18 us -> 5.56 us
  starting transfers between devices: 42 us -> 35.5 us
    dot_general x24 -> x0, matrix products: 57.5 us -> none  [the longest x4 21.3 us: shard_term(): return jnp.dot(hidden, down_rows, preferred_element_type=jnp.float32)]
    pallas_call x0 -> x8, Pallas kernels: none -> 24.2 us  [the longest x4 18.5 us: attend(): pl.pallas_call(functools.partial(attend_kernel, back, last), out_shape=ou...]
    ppermute x15, waiting for transfers between devices: 18 us -> 5.56 us  [the longest x6 5.54 us: to_next(): return lax.ppermute(value, 'blk', [(i, i + 1) for i in range(count - 1)])]
    reduce_sum x9 -> x0, other arithmetic: 10.3 us -> none  [the longest x8 7.21 us: group_of_head(): denominator = jnp.sum(weights, axis=-1, keepdims=True)]
    dynamic_slice x16 -> x0, local copies, waits for them, and re-layouts: 8.85 us -> none  [group_of_head(): lax.dynamic_slice_in_dim(query_states, group_index * heads_per_group * HE...]
    ppermute x15, starting transfers between devices: 42 us -> 35.5 us  [the longest x9 21.9 us: to_previous(): lax.ppermute(value, 'blk', [(i, (i - 1) % count) for i in range(count)])]
    unnamed x19 -> x22, local copies, waits for them, and re-layouts: 9.54 us -> 6.22 us
    concatenate x2 -> x0, other arithmetic: 3.1 us -> none  [the longest x1 1.61 us: per_device(): jnp.concatenate([block_pair[1] for block_pair in ordered], axis=0)]
  transfers between devices with their start and end apart: 15 -> 15, of which waited for: 3 -> 2; matrix products, arithmetic and copies ran while one was open for 56% -> 0% of each run, Pallas kernels for 0% -> 31%
where the time goes in v1:
time: 72.8 us; the launch traced here: 72.3 us
  starting transfers between devices  35.5 us (49%)
  Pallas kernels  24.2 us (33%)
  local copies, waits for them, and re-layouts  6.22 us (9%)
  waiting for transfers between devices  5.56 us (8%)
  between operations  0.85 us (1%)
    ppermute x9, starting transfers between devices, to_previous(): lax.ppermute(value, 'blk', [(i, (i - 1) % count) for i in range(count)])  21.9 us
    pallas_call x4, Pallas kernels, attend(): pl.pallas_call(functools.partial(attend_kernel, back, last), out_shape=ou...  18.5 us
    ppermute x6, starting transfers between devices, to_next(): return lax.ppermute(value, 'blk', [(i, i + 1) for i in range(count - 1)])  13.6 us
    unnamed x22, local copies, waits for them, and re-layouts  6.22 us
    ppermute x6, waiting for transfers between devices, to_next(): return lax.ppermute(value, 'blk', [(i, i + 1) for i in range(count - 1)])  5.54 us
    pallas_call x1, Pallas kernels, down(): pl.pallas_call(functools.partial(down_kernel, slot), out_shape=jax.ShapeD...  2.05 us
    pallas_call x2, Pallas kernels, gate_up(): pl.pallas_call(functools.partial(gate_kernel, shards, slot), out_shape=ja...  1.88 us
    pallas_call x1, Pallas kernels, normed_rows(): pl.pallas_call(normed_kernel, out_shape=jax.ShapeDtypeStruct((rows, featu...  1.74 us
  transfers between devices with their start and end apart: 15, of which 2 were waited for; matrix products, arithmetic and copies ran while one was open for 0% of the time, Pallas kernels for 31%

profile of v1, /device:TPU:6, one launch (start us, length us, event | category | flops | bytes accessed | tf_op | source)
XLA Modules:
  0.0 72.3 jit_solution(6888870701605683552)
XLA Ops:
  0.6 0.0 copy-start.8
  0.6 1.9 %collective-permute-start.2 = (bf16[256,1024]{1,0:T(8,128)(2,1)}, bf16[256,1024]{1,0:T(8,128)(2,1)S(1)}, u32[]{:S(2)}, u32[]{:S(2)}) collective-permute-start(bf16[256,1024]{1,0:T(8,128)(2,1)} %refs_2_.3), channel_id=1, source_target_pairs={{0,1},{1,2},{2,3},{3,4},{4,5},{5,6},{6,7},{7,8},{8,9},{9,10},{10,1... | collective-permute-start | bytes 1572872 | tf_op jit(solution)/shard_map/ppermute | solution.py:25
  2.6 3.6 %collective-permute-start = (bf16[256,1024]{1,0:T(8,128)(2,1)}, bf16[256,1024]{1,0:T(8,128)(2,1)S(1)}, u32[]{:S(2)}, u32[]{:S(2)}) collective-permute-start(bf16[256,1024]{1,0:T(8,128)(2,1)} %refs_1_.2), channel_id=1, source_target_pairs={{0,1},{1,2},{2,3},{3,4},{4,5},{5,6},{6,7},{7,8},{8,9},{9,10},{10,1... | collective-permute-start | bytes 1572872 | tf_op jit(solution)/shard_map/ppermute | solution.py:25
  6.2 6.4 %collective-permute-start.6 = (bf16[56,4096]{1,0:T(8,128)(2,1)}, bf16[56,4096]{1,0:T(8,128)(2,1)S(1)}, u32[]{:S(2)}, u32[]{:S(2)}) collective-permute-start(bf16[56,4096]{1,0:T(8,128)(2,1)} %refs_1_.3), channel_id=1, source_target_pairs={{0,255},{1,0},{2,1},{3,2},{4,3},{5,4},{6,5},{7,6},{8,7},{9,8},{10,... | collective-permute-start | bytes 1376264 | tf_op jit(solution)/shard_map/ppermute | solution.py:30
  12.6 0.7 collective-permute-start.7
  13.3 1.7 %collective-permute-start.12 = (bf16[56,4096]{1,0:T(8,128)(2,1)}, bf16[56,4096]{1,0:T(8,128)(2,1)S(1)}, u32[]{:S(2)}, u32[]{:S(2)}) collective-permute-start(bf16[56,4096]{1,0:T(8,128)(2,1)} %refs_2_.5), channel_id=1, source_target_pairs={{0,255},{1,0},{2,1},{3,2},{4,3},{5,4},{6,5},{7,6},{8,7},{9,8},{10,... | collective-permute-start | bytes 1376264 | tf_op jit(solution)/shard_map/ppermute | solution.py:30
  15.0 0.0 copy-start
  15.0 1.6 %copy-done = bf16[256,4096]{1,0:T(8,128)(2,1)S(1)} copy-done((bf16[256,4096]{1,0:T(8,128)(2,1)S(1)}, bf16[256,4096]{1,0:T(8,128)(2,1)}, u32[]{:S(2)}) %copy-start) | copy-done | bytes 2097176
  16.6 0.0 copy-start.7
  16.6 0.7 copy-done.7
  17.3 0.0 copy-start.9
  17.3 1.0 %copy-done.9 = bf16[256,1024]{1,0:T(8,128)(2,1)S(1)} copy-done((bf16[256,1024]{1,0:T(8,128)(2,1)S(1)}, bf16[256,1024]{1,0:T(8,128)(2,1)}, u32[]{:S(2)}) %copy-start.9) | copy-done | bytes 524312
  18.3 0.0 copy-start.10
  18.3 1.0 %copy-done.10 = bf16[256,1024]{1,0:T(8,128)(2,1)S(1)} copy-done((bf16[256,1024]{1,0:T(8,128)(2,1)S(1)}, bf16[256,1024]{1,0:T(8,128)(2,1)}, u32[]{:S(2)}) %copy-start.10) | copy-done | bytes 524312
  19.4 3.8 %attend_0.1 = (f32[8,8,256]{2,1,0:T(8,128)S(1)}, f32[8,512,256]{2,1,0:T(8,128)S(1)}) custom-call(bf16[256,4096]{1,0:T(8,128)(2,1)S(1)} %copy-done, bf16[256,1024]{1,0:T(8,128)(2,1)S(1)} %copy-done.10, bf16[256,1024]{1,0:T(8,128)(2,1)S(1)} %copy-done.9, s32[1,256]{1,0:T(1,128)S(1)} %bitcast.3), custom_call_target="tpu_custom_call" | custom-call | flops 1073741824 | bytes 12582912 | tf_op jit(solution)/shard_map/attend_0/pallas_call | solution.py:95
  23.2 0.0 collective-permute-done.2.refs_2_
  23.2 1.9 %collective-permute-start.4 = (bf16[256,1024]{1,0:T(8,128)(2,1)S(1)}, bf16[256,1024]{1,0:T(8,128)(2,1)S(1)}, u32[]{:S(2)}, u32[]{:S(2)}) collective-permute-start(bf16[256,1024]{1,0:T(8,128)(2,1)S(1)} %collective-permute-done.2.refs_2_), channel_id=1, source_target_pairs={{0,1},{1,2},{2,3},{3,4},{4,5},{5,6},{6,7},{7,8},{8,9},{9,10},{10,1... | collective-permute-start | bytes 1572872 | tf_op jit(solution)/shard_map/ppermute | solution.py:25
  25.1 0.0 collective-permute-done.refs_1_
  25.2 1.9 %collective-permute-start.1 = (bf16[256,1024]{1,0:T(8,128)(2,1)S(1)}, bf16[256,1024]{1,0:T(8,128)(2,1)S(1)}, u32[]{:S(2)}, u32[]{:S(2)}) collective-permute-start(bf16[256,1024]{1,0:T(8,128)(2,1)S(1)} %collective-permute-done.refs_1_), channel_id=1, source_target_pairs={{0,1},{1,2},{2,3},{3,4},{4,5},{5,6},{6,7},{7,8},{8,9},{9,10},{10,1... | collective-permute-start | bytes 1572872 | tf_op jit(solution)/shard_map/ppermute | solution.py:25
  27.1 0.0 collective-permute-done.6.refs_3_
  27.1 6.0 %collective-permute-start.8 = (bf16[56,4096]{1,0:T(8,128)(2,1)S(1)}, bf16[56,4096]{1,0:T(8,128)(2,1)S(1)}, u32[]{:S(2)}, u32[]{:S(2)}) collective-permute-start(bf16[56,4096]{1,0:T(8,128)(2,1)S(1)} %collective-permute-done.6.refs_3_), channel_id=1, source_target_pairs={{0,255},{1,0},{2,1},{3,2},{4,3},{5,4},{6,5},{7,6},{8,7},{9,8},{10,... | collective-permute-start | bytes 1376264 | tf_op jit(solution)/shard_map/ppermute | solution.py:30
  33.1 0.0 collective-permute-done.7.refs_4_
  33.1 0.5 collective-permute-start.9
  33.6 0.0 copy-done.8
  33.6 4.1 %attend_1.1 = (f32[8,8,256]{2,1,0:T(8,128)S(1)}, f32[8,512,256]{2,1,0:T(8,128)S(1)}) custom-call(bf16[256,4096]{1,0:T(8,128)(2,1)S(1)} %copy-done, bf16[256,1024]{1,0:T(8,128)(2,1)S(1)} %collective-permute-done.refs_1_, bf16[256,1024]{1,0:T(8,128)(2,1)S(1)} %collective-permute-done.2.refs_2_, s32[1,256]{1,0:T(1,128)S(1)} %bitcast.4, ...), custom_call_target="tpu_custom_call" | custom-call | flops 1073741824 | bytes 12582912 | tf_op jit(solution)/shard_map/attend_1/pallas_call | solution.py:95
  37.8 0.0 collective-permute-done.12.refs_3_
  37.8 0.2 collective-permute-start.13
  38.0 0.0 collective-permute-done.4.refs_2_
  38.0 2.3 %collective-permute-start.5 = (bf16[256,1024]{1,0:T(8,128)(2,1)S(1)}, bf16[256,1024]{1,0:T(8,128)(2,1)S(1)}, u32[]{:S(2)}, u32[]{:S(2)}) collective-permute-start(bf16[256,1024]{1,0:T(8,128)(2,1)S(1)} %collective-permute-done.4.refs_2_), channel_id=1, source_target_pairs={{0,1},{1,2},{2,3},{3,4},{4,5},{5,6},{6,7},{7,8},{8,9},{9,10},{10,1... | collective-permute-start | bytes 1572872 | tf_op jit(solution)/shard_map/ppermute | solution.py:25
  40.3 3.3 %collective-permute-done.1.refs_1_ = bf16[256,1024]{1,0:T(8,128)(2,1)S(1)} collective-permute-done((bf16[256,1024]{1,0:T(8,128)(2,1)S(1)}, bf16[256,1024]{1,0:T(8,128)(2,1)S(1)}, u32[]{:S(2)}, u32[]{:S(2)}) %collective-permute-start.1) | collective-permute-done | bytes 524320 | tf_op jit(solution)/shard_map/ppermute | solution.py:25
  43.6 1.9 %collective-permute-start.3 = (bf16[256,1024]{1,0:T(8,128)(2,1)S(1)}, bf16[256,1024]{1,0:T(8,128)(2,1)S(1)}, u32[]{:S(2)}, u32[]{:S(2)}) collective-permute-start(bf16[256,1024]{1,0:T(8,128)(2,1)S(1)} %collective-permute-done.1.refs_1_), channel_id=1, source_target_pairs={{0,1},{1,2},{2,3},{3,4},{4,5},{5,6},{6,7},{7,8},{8,9},{9,10},{10,1... | collective-permute-start | bytes 1572872 | tf_op jit(solution)/shard_map/ppermute | solution.py:25
  45.5 0.0 collective-permute-done.8.refs_5_
  45.5 6.0 %collective-permute-start.10 = (bf16[56,4096]{1,0:T(8,128)(2,1)S(1)}, bf16[56,4096]{1,0:T(8,128)(2,1)S(1)}, u32[]{:S(2)}, u32[]{:S(2)}) collective-permute-start(bf16[56,4096]{1,0:T(8,128)(2,1)S(1)} %collective-permute-done.8.refs_5_), channel_id=1, source_target_pairs={{0,255},{1,0},{2,1},{3,2},{4,3},{5,4},{6,5},{7,6},{8,7},{9,8},{10,... | collective-permute-start | bytes 1376264 | tf_op jit(solution)/shard_map/ppermute | solution.py:30
  51.5 4.1 %attend_2.1 = (f32[8,8,256]{2,1,0:T(8,128)S(1)}, f32[8,512,256]{2,1,0:T(8,128)S(1)}) custom-call(bf16[256,4096]{1,0:T(8,128)(2,1)S(1)} %copy-done, bf16[256,1024]{1,0:T(8,128)(2,1)S(1)} %collective-permute-done.1.refs_1_, bf16[256,1024]{1,0:T(8,128)(2,1)S(1)} %collective-permute-done.4.refs_2_, s32[1,256]{1,0:T(1,128)S(1)} %bitcast.5, ...), custom_call_target="tpu_custom_call" | custom-call | flops 1073741824 | bytes 12582912 | tf_op jit(solution)/shard_map/attend_2/pallas_call | solution.py:95
  55.6 0.0 collective-permute-done.9.refs_6_
  55.7 0.3 collective-permute-start.11
  55.9 0.0 collective-permute-done.13.refs_4_
  55.9 0.1 collective-permute-start.14
  56.0 0.0 collective-permute-done.5.refs_2_
  56.0 2.2 %collective-permute-done.3.refs_1_ = bf16[256,1024]{1,0:T(8,128)(2,1)S(1)} collective-permute-done((bf16[256,1024]{1,0:T(8,128)(2,1)S(1)}, bf16[256,1024]{1,0:T(8,128)(2,1)S(1)}, u32[]{:S(2)}, u32[]{:S(2)}) %collective-permute-start.3) | collective-permute-done | bytes 524320 | tf_op jit(solution)/shard_map/ppermute | solution.py:25
  58.3 0.0 copy-start.2
  58.3 0.0 copy-start.6
  58.3 6.4 %attend_3.1.attended_ref = bf16[256,4096]{1,0:T(8,128)(2,1)} custom-call(bf16[256,4096]{1,0:T(8,128)(2,1)S(1)} %copy-done, bf16[256,1024]{1,0:T(8,128)(2,1)S(1)} %collective-permute-done.3.refs_1_, bf16[256,1024]{1,0:T(8,128)(2,1)S(1)} %collective-permute-done.5.refs_2_, s32[1,256]{1,0:T(1,128)S(1)} %bitcast.6, f32[8,8,256]{2,1,0:T(8,128)S(1)} %get-tuple-element.26.refs_4_, ...), custom_call_target="tpu_custom_call" | custom-call | flops 1073741824 | bytes 12582912 | tf_op jit(solution)/shard_map/attend_3/pallas_call | solution.py:95
  64.7 0.0 copy-done.2
  64.7 0.0 copy-done.6
  64.7 0.0 copy-start.1
  64.7 1.6 %copy-done.1 = bf16[256,4096]{1,0:T(8,128)(2,1)S(1)} copy-done((bf16[256,4096]{1,0:T(8,128)(2,1)S(1)}, bf16[256,4096]{1,0:T(8,128)(2,1)}, u32[]{:S(2)}) %copy-start.1) | copy-done | bytes 2097176
  66.3 1.7 %norm.1.refs_0_ = bf16[256,4096]{1,0:T(8,128)(2,1)S(1)} custom-call(bf16[256,4096]{1,0:T(8,128)(2,1)S(1)} %copy-done.1, bf16[256,4096]{1,0:T(8,128)(2,1)S(1)} %copy-done.2, f32[1,4096]{1,0:T(1,128)S(1)} %bitcast.2), custom_call_target="tpu_custom_call" | custom-call | flops 6291456 | bytes 6291456 | tf_op jit(solution)/shard_map/norm/pallas_call | solution.py:154
  68.0 0.0 copy-start.3
  68.1 0.0 copy-start.4
  68.1 0.0 collective-permute-done.10.refs_1_
  68.1 0.0 collective-permute-done.11.refs_2_
  68.1 0.9 %gate_up_1.1.refs_1_ = bf16[64,256]{1,0:T(8,128)(2,1)S(1)} custom-call(bf16[256,4096]{1,0:T(8,128)(2,1)S(1)} %norm.1.refs_0_, bf16[56,4096]{1,0:T(8,128)(2,1)S(1)} %collective-permute-done.10.refs_1_, bf16[56,4096]{1,0:T(8,128)(2,1)S(1)} %collective-permute-done.11.refs_2_), custom_call_target="tpu_custom_call" | custom-call | flops 234881024 | bytes 3014656 | tf_op jit(solution)/shard_map/gate_up_1/pallas_call | solution.py:168
  69.0 0.1 copy-done.3
  69.1 0.1 copy-done.4
  69.2 0.0 copy-start.5
  69.2 1.0 %gate_up_3.1.refs_0_ = bf16[192,256]{1,0:T(8,128)(2,1)S(1)} custom-call(bf16[256,4096]{1,0:T(8,128)(2,1)S(1)} %norm.1.refs_0_, bf16[56,4096]{1,0:T(8,128)(2,1)S(1)} %copy-done.3, bf16[56,4096]{1,0:T(8,128)(2,1)S(1)} %copy-done.4, bf16[56,4096]{1,0:T(8,128)(2,1)S(1)} %collective-permute-done.6.refs_3_, bf16[56,4096]{1,0:T(8,128)(2,1)S(1)} %collective-permute-done.7.refs_4_, ...), custom_call_target="tpu_custom_call" | custom-call | flops 704643072 | bytes 4849664 | tf_op jit(solution)/shard_map/gate_up_3/pallas_call | solution.py:168
  70.2 0.0 collective-permute-done.14.refs_5_
  70.3 0.0 copy-done.5
  70.3 2.1 %down.1 = bf16[256,4096]{1,0:T(8,128)(2,1)} custom-call(bf16[192,256]{1,0:T(8,128)(2,1)S(1)} %gate_up_3.1.refs_0_, bf16[64,256]{1,0:T(8,128)(2,1)S(1)} %gate_up_1.1.refs_1_, bf16[56,4096]{1,0:T(8,128)(2,1)S(1)} %copy-done.5, bf16[56,4096]{1,0:T(8,128)(2,1)S(1)} %collective-permute-done.12.refs_3_, bf16[56,4096]{1,0:T(8,128)(2,1)S(1)} %collective-permute-done.13.refs_4_, ...), custom_call_target="tpu_custom_call" | custom-call | flops 469762048 | bytes 4194304 | tf_op jit(solution)/shard_map/down/pallas_call | solution.py:186
Async XLA Ops:
  0.6 33.0 %copy-start.8 = (s32[256]{0:T(256)S(1)}, s32[256]{0:T(256)}, u32[]{:S(2)}) copy-start(s32[256]{0:T(256)} %param.12) | copy-start | bytes 3076
  0.6 22.6 %collective-permute-start.2 = (bf16[256,1024]{1,0:T(8,128)(2,1)}, bf16[256,1024]{1,0:T(8,128)(2,1)S(1)}, u32[]{:S(2)}, u32[]{:S(2)}) collective-permute-start(bf16[256,1024]{1,0:T(8,128)(2,1)} %refs_2_.3), channel_id=1, source_target_pairs={{0,1},{1,2},{2,3},{3,4},{4,5},{5,6},{6,7},{7,8},{8,9},{9,10},{10,1... | collective-permute-start | bytes 1572872 | tf_op jit(solution)/shard_map/ppermute | solution.py:25
  2.6 22.6 %collective-permute-start = (bf16[256,1024]{1,0:T(8,128)(2,1)}, bf16[256,1024]{1,0:T(8,128)(2,1)S(1)}, u32[]{:S(2)}, u32[]{:S(2)}) collective-permute-start(bf16[256,1024]{1,0:T(8,128)(2,1)} %refs_1_.2), channel_id=1, source_target_pairs={{0,1},{1,2},{2,3},{3,4},{4,5},{5,6},{6,7},{7,8},{8,9},{9,10},{10,1... | collective-permute-start | bytes 1572872 | tf_op jit(solution)/shard_map/ppermute | solution.py:25
  6.2 20.9 %collective-permute-start.6 = (bf16[56,4096]{1,0:T(8,128)(2,1)}, bf16[56,4096]{1,0:T(8,128)(2,1)S(1)}, u32[]{:S(2)}, u32[]{:S(2)}) collective-permute-start(bf16[56,4096]{1,0:T(8,128)(2,1)} %refs_1_.3), channel_id=1, source_target_pairs={{0,255},{1,0},{2,1},{3,2},{4,3},{5,4},{6,5},{7,6},{8,7},{9,8},{10,... | collective-permute-start | bytes 1376264 | tf_op jit(solution)/shard_map/ppermute | solution.py:30
  12.6 20.5 %collective-permute-start.7 = (bf16[56,4096]{1,0:T(8,128)(2,1)}, bf16[56,4096]{1,0:T(8,128)(2,1)S(1)}, u32[]{:S(2)}, u32[]{:S(2)}) collective-permute-start(bf16[56,4096]{1,0:T(8,128)(2,1)} %refs_2_.4), channel_id=1, source_target_pairs={{0,255},{1,0},{2,1},{3,2},{4,3},{5,4},{6,5},{7,6},{8,7},{9,8},{10,... | collective-permute-start | bytes 1376264 | tf_op jit(solution)/shard_map/ppermute | solution.py:30
  13.3 24.5 %collective-permute-start.12 = (bf16[56,4096]{1,0:T(8,128)(2,1)}, bf16[56,4096]{1,0:T(8,128)(2,1)S(1)}, u32[]{:S(2)}, u32[]{:S(2)}) collective-permute-start(bf16[56,4096]{1,0:T(8,128)(2,1)} %refs_2_.5), channel_id=1, source_target_pairs={{0,255},{1,0},{2,1},{3,2},{4,3},{5,4},{6,5},{7,6},{8,7},{9,8},{10,... | collective-permute-start | bytes 1376264 | tf_op jit(solution)/shard_map/ppermute | solution.py:30
  15.0 1.6 %copy-start = (bf16[256,4096]{1,0:T(8,128)(2,1)S(1)}, bf16[256,4096]{1,0:T(8,128)(2,1)}, u32[]{:S(2)}) copy-start(bf16[256,4096]{1,0:T(8,128)(2,1)} %refs_0_.7) | copy-start | bytes 6291460
  16.6 0.7 copy-start.7
  17.3 1.0 %copy-start.9 = (bf16[256,1024]{1,0:T(8,128)(2,1)S(1)}, bf16[256,1024]{1,0:T(8,128)(2,1)}, u32[]{:S(2)}) copy-start(bf16[256,1024]{1,0:T(8,128)(2,1)} %refs_2_.3) | copy-start | bytes 1572868
  18.3 1.0 %copy-start.10 = (bf16[256,1024]{1,0:T(8,128)(2,1)S(1)}, bf16[256,1024]{1,0:T(8,128)(2,1)}, u32[]{:S(2)}) copy-start(bf16[256,1024]{1,0:T(8,128)(2,1)} %refs_1_.2) | copy-start | bytes 1572868
  23.2 14.7 %collective-permute-start.4 = (bf16[256,1024]{1,0:T(8,128)(2,1)S(1)}, bf16[256,1024]{1,0:T(8,128)(2,1)S(1)}, u32[]{:S(2)}, u32[]{:S(2)}) collective-permute-start(bf16[256,1024]{1,0:T(8,128)(2,1)S(1)} %collective-permute-done.2.refs_2_), channel_id=1, source_target_pairs={{0,1},{1,2},{2,3},{3,4},{4,5},{5,6},{6,7},{7,8},{8,9},{9,10},{10,1... | collective-permute-start | bytes 1572872 | tf_op jit(solution)/shard_map/ppermute | solution.py:25
  25.2 18.4 %collective-permute-start.1 = (bf16[256,1024]{1,0:T(8,128)(2,1)S(1)}, bf16[256,1024]{1,0:T(8,128)(2,1)S(1)}, u32[]{:S(2)}, u32[]{:S(2)}) collective-permute-start(bf16[256,1024]{1,0:T(8,128)(2,1)S(1)} %collective-permute-done.refs_1_), channel_id=1, source_target_pairs={{0,1},{1,2},{2,3},{3,4},{4,5},{5,6},{6,7},{7,8},{8,9},{9,10},{10,1... | collective-permute-start | bytes 1572872 | tf_op jit(solution)/shard_map/ppermute | solution.py:25
  27.1 18.4 %collective-permute-start.8 = (bf16[56,4096]{1,0:T(8,128)(2,1)S(1)}, bf16[56,4096]{1,0:T(8,128)(2,1)S(1)}, u32[]{:S(2)}, u32[]{:S(2)}) collective-permute-start(bf16[56,4096]{1,0:T(8,128)(2,1)S(1)} %collective-permute-done.6.refs_3_), channel_id=1, source_target_pairs={{0,255},{1,0},{2,1},{3,2},{4,3},{5,4},{6,5},{7,6},{8,7},{9,8},{10,... | collective-permute-start | bytes 1376264 | tf_op jit(solution)/shard_map/ppermute | solution.py:30
  33.1 22.5 %collective-permute-start.9 = (bf16[56,4096]{1,0:T(8,128)(2,1)S(1)}, bf16[56,4096]{1,0:T(8,128)(2,1)S(1)}, u32[]{:S(2)}, u32[]{:S(2)}) collective-permute-start(bf16[56,4096]{1,0:T(8,128)(2,1)S(1)} %collective-permute-done.7.refs_4_), channel_id=1, source_target_pairs={{0,255},{1,0},{2,1},{3,2},{4,3},{5,4},{6,5},{7,6},{8,7},{9,8},{10,... | collective-permute-start | bytes 1376264 | tf_op jit(solution)/shard_map/ppermute | solution.py:30
  37.8 18.2 %collective-permute-start.13 = (bf16[56,4096]{1,0:T(8,128)(2,1)S(1)}, bf16[56,4096]{1,0:T(8,128)(2,1)S(1)}, u32[]{:S(2)}, u32[]{:S(2)}) collective-permute-start(bf16[56,4096]{1,0:T(8,128)(2,1)S(1)} %collective-permute-done.12.refs_3_), channel_id=1, source_target_pairs={{0,255},{1,0},{2,1},{3,2},{4,3},{5,4},{6,5},{7,6},{8,7},{9,8},{10,... | collective-permute-start | bytes 1376264 | tf_op jit(solution)/shard_map/ppermute | solution.py:30
  38.0 18.1 %collective-permute-start.5 = (bf16[256,1024]{1,0:T(8,128)(2,1)S(1)}, bf16[256,1024]{1,0:T(8,128)(2,1)S(1)}, u32[]{:S(2)}, u32[]{:S(2)}) collective-permute-start(bf16[256,1024]{1,0:T(8,128)(2,1)S(1)} %collective-permute-done.4.refs_2_), channel_id=1, source_target_pairs={{0,1},{1,2},{2,3},{3,4},{4,5},{5,6},{6,7},{7,8},{8,9},{9,10},{10,1... | collective-permute-start | bytes 1572872 | tf_op jit(solution)/shard_map/ppermute | solution.py:25
  43.6 14.7 %collective-permute-start.3 = (bf16[256,1024]{1,0:T(8,128)(2,1)S(1)}, bf16[256,1024]{1,0:T(8,128)(2,1)S(1)}, u32[]{:S(2)}, u32[]{:S(2)}) collective-permute-start(bf16[256,1024]{1,0:T(8,128)(2,1)S(1)} %collective-permute-done.1.refs_1_), channel_id=1, source_target_pairs={{0,1},{1,2},{2,3},{3,4},{4,5},{5,6},{6,7},{7,8},{8,9},{9,10},{10,1... | collective-permute-start | bytes 1572872 | tf_op jit(solution)/shard_map/ppermute | solution.py:25
  45.5 22.6 %collective-permute-start.10 = (bf16[56,4096]{1,0:T(8,128)(2,1)S(1)}, bf16[56,4096]{1,0:T(8,128)(2,1)S(1)}, u32[]{:S(2)}, u32[]{:S(2)}) collective-permute-start(bf16[56,4096]{1,0:T(8,128)(2,1)S(1)} %collective-permute-done.8.refs_5_), channel_id=1, source_target_pairs={{0,255},{1,0},{2,1},{3,2},{4,3},{5,4},{6,5},{7,6},{8,7},{9,8},{10,... | collective-permute-start | bytes 1376264 | tf_op jit(solution)/shard_map/ppermute | solution.py:30
  55.7 12.4 %collective-permute-start.11 = (bf16[56,4096]{1,0:T(8,128)(2,1)S(1)}, bf16[56,4096]{1,0:T(8,128)(2,1)S(1)}, u32[]{:S(2)}, u32[]{:S(2)}) collective-permute-start(bf16[56,4096]{1,0:T(8,128)(2,1)S(1)} %collective-permute-done.9.refs_6_), channel_id=1, source_target_pairs={{0,255},{1,0},{2,1},{3,2},{4,3},{5,4},{6,5},{7,6},{8,7},{9,8},{10,... | collective-permute-start | bytes 1376264 | tf_op jit(solution)/shard_map/ppermute | solution.py:30
  55.9 14.3 %collective-permute-start.14 = (bf16[56,4096]{1,0:T(8,128)(2,1)S(1)}, bf16[56,4096]{1,0:T(8,128)(2,1)S(1)}, u32[]{:S(2)}, u32[]{:S(2)}) collective-permute-start(bf16[56,4096]{1,0:T(8,128)(2,1)S(1)} %collective-permute-done.13.refs_4_), channel_id=1, source_target_pairs={{0,255},{1,0},{2,1},{3,2},{4,3},{5,4},{6,5},{7,6},{8,7},{9,8},{10,... | collective-permute-start | bytes 1376264 | tf_op jit(solution)/shard_map/ppermute | solution.py:30
  58.3 6.4 %copy-start.2 = (bf16[256,4096]{1,0:T(8,128)(2,1)S(1)}, bf16[256,4096]{1,0:T(8,128)(2,1)}, u32[]{:S(2)}) copy-start(bf16[256,4096]{1,0:T(8,128)(2,1)} %residual_ref.1) | copy-start | bytes 6291460
  58.3 6.4 %copy-start.6 = (f32[4096]{0:T(1024)S(1)}, f32[4096]{0:T(1024)}, u32[]{:S(2)}) copy-start(f32[4096]{0:T(1024)} %param.14) | copy-start | bytes 49156
  64.7 1.6 %copy-start.1 = (bf16[256,4096]{1,0:T(8,128)(2,1)S(1)}, bf16[256,4096]{1,0:T(8,128)(2,1)}, u32[]{:S(2)}) copy-start(bf16[256,4096]{1,0:T(8,128)(2,1)} %attend_3.1.attended_ref) | copy-start | bytes 6291460
  68.0 1.0 %copy-start.3 = (bf16[56,4096]{1,0:T(8,128)(2,1)S(1)}, bf16[56,4096]{1,0:T(8,128)(2,1)}, u32[]{:S(2)}) copy-start(bf16[56,4096]{1,0:T(8,128)(2,1)} %refs_1_.3) | copy-start | bytes 1376260
  68.1 1.1 %copy-start.4 = (bf16[56,4096]{1,0:T(8,128)(2,1)S(1)}, bf16[56,4096]{1,0:T(8,128)(2,1)}, u32[]{:S(2)}) copy-start(bf16[56,4096]{1,0:T(8,128)(2,1)} %refs_2_.4) | copy-start | bytes 1376260
  69.2 1.0 %copy-start.5 = (bf16[56,4096]{1,0:T(8,128)(2,1)S(1)}, bf16[56,4096]{1,0:T(8,128)(2,1)}, u32[]{:S(2)}) copy-start(bf16[56,4096]{1,0:T(8,128)(2,1)} %refs_2_.5) | copy-start | bytes 1376260

commit v2 on v1

--- a/solution.py
+++ b/solution.py
@@ -22,7 +22,7 @@
 
 def to_next(value):
     count = lax.axis_size("blk")
-    return lax.ppermute(value, "blk", [(i, i + 1) for i in range(count - 1)])
+    return lax.ppermute(value, "blk", [(i, (i + 1) % count) for i in range(count)])
 
 
 def to_previous(value):
@@ -35,11 +35,21 @@
 
 
 def attend_kernel(back, last, *refs):
-    q_ref, k_ref, v_ref, position_ref = refs[:4]
-    if back > 0:
-        stat_ref, sum_ref = refs[4:6]
-    bias_ref = refs[-1]
-    out = refs[4 if back == 0 else 6 : -1]
+    if back == 0:
+        q_ref, k_ref, v_ref, position_ref = refs[:4]
+        *out, bias_ref = refs[4:]
+    else:
+        q_ref, k_ref, v_ref, position_ref, stat_ref, sum_ref = refs[:6]
+        if last:
+            residual_ref, gain_ref, attended_out, normed_ref, bias_ref, attended_ref, semaphores = refs[6:]
+        else:
+            *out, bias_ref = refs[6:]
+
+    def attended_copy(index):
+        wide = GROUP * HEAD_SIZE
+        columns = pl.ds(pl.multiple_of(index * wide, wide), wide)
+        return pltpu.make_async_copy(attended_ref.at[:, columns], attended_out.at[:, columns], semaphores.at[index])
+
     rows = q_ref.shape[0]
     key = lax.broadcasted_iota(jnp.int32, (rows, rows), 0) - back * rows
     query = lax.broadcasted_iota(jnp.int32, (rows, rows), 1)
@@ -73,29 +83,48 @@
                     total = total + stat_ref[index, GROUP + head : GROUP + head + 1, some] * shrink
                     mixed = mixed + sum_ref[index, features, some] * shrink
                 if last:
-                    out[0][some, columns] = (mixed * (1.0 / total)).T.astype(jnp.bfloat16)
+                    attended_ref[some, columns] = (mixed * (1.0 / total)).T.astype(jnp.bfloat16)
                 else:
                     out[0][index, head : head + 1, some] = top
                     out[0][index, GROUP + head : GROUP + head + 1, some] = total
                     out[1][index, features, some] = mixed
+        if last:
+            attended_copy(index).start()
         return 0
 
     lax.fori_loop(0, KEY_VALUE_HEADS, group, 0, unroll=4)
+    if last:
+        normed_rows(attended_ref, residual_ref, gain_ref, normed_ref)
+        for index in range(KEY_VALUE_HEADS):
+            attended_copy(index).wait()
 
 
 def attend(back, last, queries, keys, values, positions, carry=()):
     rows = queries.shape[0]
+    out_specs = None
     if last:
-        out_shape = (jax.ShapeDtypeStruct(queries.shape, jnp.bfloat16),)
+        out_shape = (jax.ShapeDtypeStruct(queries.shape, jnp.bfloat16),) * 2
+        out_specs = (pl.BlockSpec(memory_space=pltpu.HBM), pl.BlockSpec(memory_space=pltpu.VMEM))
     else:
         out_shape = (
             jax.ShapeDtypeStruct((KEY_VALUE_HEADS, 2 * GROUP, rows), jnp.float32),
             jax.ShapeDtypeStruct((KEY_VALUE_HEADS, GROUP * HEAD_SIZE, rows), jnp.float32),
         )
+    scratch_shapes = [pltpu.VMEM((rows, rows), jnp.float32)]
+    in_specs = [pl.BlockSpec(memory_space=pltpu.VMEM)] * (4 + len(carry))
+    if last:
+        scratch_shapes += [
+            pltpu.VMEM(queries.shape, jnp.bfloat16),
+            pltpu.SemaphoreType.DMA((KEY_VALUE_HEADS,)),
+        ]
+    if out_specs is None:
+        out_specs = (pl.BlockSpec(memory_space=pltpu.VMEM),) * len(out_shape)
     return pl.pallas_call(
         functools.partial(attend_kernel, back, last),
         out_shape=out_shape,
-        scratch_shapes=[pltpu.VMEM((rows, rows), jnp.float32)],
+        in_specs=in_specs,
+        out_specs=out_specs,
+        scratch_shapes=scratch_shapes,
         name=f"attend_{back}",
         compiler_params=pltpu.CompilerParams(vmem_limit_bytes=16 << 20),
         cost_estimate=pl.CostEstimate(
@@ -106,7 +135,7 @@
     )(queries, keys, values, positions, *carry)
 
 
-def normed_kernel(attended_ref, residual_ref, gain_ref, out_ref):
+def normed_rows(attended_ref, residual_ref, gain_ref, out_ref):
     step = 16
 
     def some(index, _):
@@ -137,27 +166,21 @@
 def down_kernel(slot, *refs):
     early_ref, late_ref = refs[:2]
     downs = refs[2 : 2 + FFN_STEPS]
-    out_ref, rhs_ref = refs[2 + FFN_STEPS :]
+    out_ref, rhs_ref, piece_ref, semaphores = refs[2 + FFN_STEPS :]
     units = downs[0].shape[0]
     for index, rows in enumerate(downs):
         rhs_ref[index * slot : index * slot + units, :] = rows[...]
         rhs_ref[index * slot + units : (index + 1) * slot, :] = jnp.zeros((slot - units, rhs_ref.shape[1]), rhs_ref.dtype)
     hidden = jnp.concatenate([early_ref[...], late_ref[...]], axis=0).T
-    width = 512
-    for start in range(0, out_ref.shape[1], width):
-        some = slice(start, start + width)
-        out_ref[:, some] = jnp.dot(hidden, rhs_ref[:, some], preferred_element_type=jnp.float32).astype(jnp.bfloat16)
-
-
-def normed_rows(attended, residual, gain):
-    rows, features = attended.shape
-    return pl.pallas_call(
-        normed_kernel,
-        out_shape=jax.ShapeDtypeStruct((rows, features), jnp.bfloat16),
-        name="norm",
-        compiler_params=pltpu.CompilerParams(vmem_limit_bytes=16 << 20),
-        cost_estimate=pl.CostEstimate(flops=6 * rows * features, transcendentals=rows, bytes_accessed=6 << 20),
-    )(attended, residual, gain)
+    width = out_ref.shape[1] // semaphores.shape[0]
+    copies = []
+    for piece in range(semaphores.shape[0]):
+        some = slice(piece * width, (piece + 1) * width)
+        piece_ref[:, some] = jnp.dot(hidden, rhs_ref[:, some], preferred_element_type=jnp.float32).astype(jnp.bfloat16)
+        copies.append(pltpu.make_async_copy(piece_ref.at[:, some], out_ref.at[:, some], semaphores.at[piece]))
+        copies[-1].start()
+    for copy in copies:
+        copy.wait()
 
 
 def gate_up(normed, *weights):
@@ -186,11 +209,16 @@
     return pl.pallas_call(
         functools.partial(down_kernel, slot),
         out_shape=jax.ShapeDtypeStruct((rows, features), jnp.bfloat16),
-        scratch_shapes=[pltpu.VMEM((FFN_STEPS * slot, features), jnp.bfloat16)],
+        out_specs=pl.BlockSpec(memory_space=pltpu.HBM),
+        scratch_shapes=[
+            pltpu.VMEM((FFN_STEPS * slot, features), jnp.bfloat16),
+            pltpu.VMEM((rows, features), jnp.bfloat16),
+            pltpu.SemaphoreType.DMA((8,)),
+        ],
         name="down",
         compiler_params=pltpu.CompilerParams(vmem_limit_bytes=16 << 20),
         cost_estimate=pl.CostEstimate(
-            flops=2 * FFN_STEPS * rows * features * units,
+            flops=64 * 2 * FFN_STEPS * rows * features * units,
             transcendentals=0,
             bytes_accessed=4 << 20,
         ),
@@ -212,11 +240,11 @@
     keys = [rotated_key_state]
     values = [value_state_rows]
     gates, ups, downs = [gate_weight], [up_weight], [down_weight]
-    keys.append(to_next(keys[0]))
-    values.append(to_next(values[0]))
     gates.append(to_previous(gates[0]))
     ups.append(to_previous(ups[0]))
     downs.append(to_previous(downs[0]))
+    keys.append(to_next(keys[0]))
+    values.append(to_next(values[0]))
 
     carry = attend(0, False, query_states, keys[0], values[0], positions)
     keys.append(to_next(after(keys[1], carry[0])))
@@ -234,8 +262,9 @@
     ups.append(to_previous(after(ups[2], carry[0])))
     downs.append(to_previous(after(downs[2], carry[0])))
 
-    (attended,) = attend(3, True, query_states, keys[3], values[3], positions, carry)
-    normed = normed_rows(attended, residual, norm_gain[None, :])
+    attended, normed = attend(
+        3, True, query_states, keys[3], values[3], positions, (*carry, residual, norm_gain[None, :])
+    )
     early = gate_up(normed, gates[0], ups[0], gates[1], ups[1], gates[2], ups[2])
     late = gate_up(normed, gates[3], ups[3])
     ffn_part = down(early, late, downs)

time: 72.8 us -> 65.4 us (0.90)
  the two profiles are of different devices: /device:TPU:6 before, /device:TPU:0 now
where the time goes in v2:
time: 65.4 us; the launch traced here: 64.4 us
  starting transfers between devices  26.6 us (41%)
  Pallas kernels  22.5 us (34%)
  waiting for transfers between devices  9.6 us (15%)
  local copies, waits for them, and re-layouts  4.65 us (7%)
  between operations  0.95 us (1%)
    ppermute x9, starting transfers between devices, to_previous(): lax.ppermute(value, 'blk', [(i, (i - 1) % count) for i in range(count)])  26.4 us
    pallas_call x4, Pallas kernels, attend(): pl.pallas_call(functools.partial(attend_kernel, back, last), out_shape=ou...  19.1 us
    ppermute x6, waiting for transfers between devices, to_next(): lax.ppermute(value, 'blk', [(i, (i + 1) % count) for i in range(count)])  9.58 us
    unnamed x20, local copies, waits for them, and re-layouts  4.65 us
    pallas_call x2, Pallas kernels, gate_up(): pl.pallas_call(functools.partial(gate_kernel, shards, slot), out_shape=ja...  1.84 us
    pallas_call x1, Pallas kernels, down(): pl.pallas_call(functools.partial(down_kernel, slot), out_shape=jax.ShapeD...  1.63 us
  transfers between devices with their start and end apart: 15, of which 4 were waited for; matrix products, arithmetic and copies ran while one was open for 0% of the time, Pallas kernels for 32%

profile of v2, /device:TPU:0, one launch (start us, length us, event | category | flops | bytes accessed | tf_op | source)
XLA Modules:
  0.0 64.4 jit_solution(750834098875864625)
XLA Ops:
  0.6 0.1 collective-permute-start
  0.7 0.1 collective-permute-start.2
  0.8 8.3 %collective-permute-start.6 = (bf16[56,4096]{1,0:T(8,128)(2,1)}, bf16[56,4096]{1,0:T(8,128)(2,1)S(1)}, u32[]{:S(2)}, u32[]{:S(2)}) collective-permute-start(bf16[56,4096]{1,0:T(8,128)(2,1)} %refs_1_.3), channel_id=1, source_target_pairs={{0,255},{1,0},{2,1},{3,2},{4,3},{5,4},{6,5},{7,6},{8,7},{9,8},{10,... | collective-permute-start | bytes 1376264 | tf_op jit(solution)/shard_map/ppermute | solution.py:30
  9.1 0.7 %collective-permute-start.7 = (bf16[56,4096]{1,0:T(8,128)(2,1)}, bf16[56,4096]{1,0:T(8,128)(2,1)S(1)}, u32[]{:S(2)}, u32[]{:S(2)}) collective-permute-start(bf16[56,4096]{1,0:T(8,128)(2,1)} %refs_2_.4), channel_id=1, source_target_pairs={{0,255},{1,0},{2,1},{3,2},{4,3},{5,4},{6,5},{7,6},{8,7},{9,8},{10,... | collective-permute-start | bytes 1376264 | tf_op jit(solution)/shard_map/ppermute | solution.py:30
  9.8 1.7 %collective-permute-start.12 = (bf16[56,4096]{1,0:T(8,128)(2,1)}, bf16[56,4096]{1,0:T(8,128)(2,1)S(1)}, u32[]{:S(2)}, u32[]{:S(2)}) collective-permute-start(bf16[56,4096]{1,0:T(8,128)(2,1)} %refs_2_.5), channel_id=1, source_target_pairs={{0,255},{1,0},{2,1},{3,2},{4,3},{5,4},{6,5},{7,6},{8,7},{9,8},{10,... | collective-permute-start | bytes 1376264 | tf_op jit(solution)/shard_map/ppermute | solution.py:30
  11.4 0.0 copy-start
  11.4 1.6 %copy-done = bf16[256,4096]{1,0:T(8,128)(2,1)S(1)} copy-done((bf16[256,4096]{1,0:T(8,128)(2,1)S(1)}, bf16[256,4096]{1,0:T(8,128)(2,1)}, u32[]{:S(2)}) %copy-start) | copy-done | bytes 2097176
  13.0 0.0 copy-start.5
  13.0 0.7 %copy-done.5 = s32[256]{0:T(256)S(1)} copy-done((s32[256]{0:T(256)S(1)}, s32[256]{0:T(256)}, u32[]{:S(2)}) %copy-start.5) | copy-done | bytes 1048
  13.7 0.0 copy-start.7
  13.7 1.0 %copy-done.7 = bf16[256,1024]{1,0:T(8,128)(2,1)S(1)} copy-done((bf16[256,1024]{1,0:T(8,128)(2,1)S(1)}, bf16[256,1024]{1,0:T(8,128)(2,1)}, u32[]{:S(2)}) %copy-start.7) | copy-done | bytes 524312
  14.7 0.0 copy-start.8
  14.7 1.0 %copy-done.8 = bf16[256,1024]{1,0:T(8,128)(2,1)S(1)} copy-done((bf16[256,1024]{1,0:T(8,128)(2,1)S(1)}, bf16[256,1024]{1,0:T(8,128)(2,1)}, u32[]{:S(2)}) %copy-start.8) | copy-done | bytes 524312
  15.8 3.8 %attend_0.1 = (f32[8,8,256]{2,1,0:T(8,128)S(1)}, f32[8,512,256]{2,1,0:T(8,128)S(1)}) custom-call(bf16[256,4096]{1,0:T(8,128)(2,1)S(1)} %copy-done, bf16[256,1024]{1,0:T(8,128)(2,1)S(1)} %copy-done.7, bf16[256,1024]{1,0:T(8,128)(2,1)S(1)} %copy-done.8, s32[1,256]{1,0:T(1,128)S(1)} %bitcast.3), custom_call_target="tpu_custom_call" | custom-call | flops 1073741824 | bytes 12582912 | tf_op jit(solution)/shard_map/attend_0/pallas_call | solution.py:122
  19.6 0.0 collective-permute-done.refs_1_
  19.6 0.1 collective-permute-start.1
  19.7 1.9 %collective-permute-done.2.refs_2_ = bf16[256,1024]{1,0:T(8,128)(2,1)S(1)} collective-permute-done((bf16[256,1024]{1,0:T(8,128)(2,1)}, bf16[256,1024]{1,0:T(8,128)(2,1)S(1)}, u32[]{:S(2)}, u32[]{:S(2)}) %collective-permute-start.2) | collective-permute-done | bytes 524320 | tf_op jit(solution)/shard_map/ppermute | solution.py:25
  21.6 0.0 collective-permute-start.4
  21.6 0.0 collective-permute-done.6.refs_3_
  21.6 7.2 %collective-permute-start.8 = (bf16[56,4096]{1,0:T(8,128)(2,1)S(1)}, bf16[56,4096]{1,0:T(8,128)(2,1)S(1)}, u32[]{:S(2)}, u32[]{:S(2)}) collective-permute-start(bf16[56,4096]{1,0:T(8,128)(2,1)S(1)} %collective-permute-done.6.refs_3_), channel_id=1, source_target_pairs={{0,255},{1,0},{2,1},{3,2},{4,3},{5,4},{6,5},{7,6},{8,7},{9,8},{10,... | collective-permute-start | bytes 1376264 | tf_op jit(solution)/shard_map/ppermute | solution.py:30
  28.8 0.0 collective-permute-done.7.refs_4_
  28.8 0.1 collective-permute-start.9
  28.9 0.0 copy-start.6
  28.9 4.1 %attend_1.1 = (f32[8,8,256]{2,1,0:T(8,128)S(1)}, f32[8,512,256]{2,1,0:T(8,128)S(1)}) custom-call(bf16[256,4096]{1,0:T(8,128)(2,1)S(1)} %copy-done, bf16[256,1024]{1,0:T(8,128)(2,1)S(1)} %collective-permute-done.refs_1_, bf16[256,1024]{1,0:T(8,128)(2,1)S(1)} %collective-permute-done.2.refs_2_, s32[1,256]{1,0:T(1,128)S(1)} %bitcast.4, ...), custom_call_target="tpu_custom_call" | custom-call | flops 1073741824 | bytes 12582912 | tf_op jit(solution)/shard_map/attend_1/pallas_call | solution.py:122
  33.0 0.0 collective-permute-done.12.refs_3_
  33.0 0.1 collective-permute-start.13
  33.1 0.6 collective-permute-done.1.refs_1_
  33.8 0.0 collective-permute-start.3
  33.8 5.6 %collective-permute-done.4.refs_2_ = bf16[256,1024]{1,0:T(8,128)(2,1)S(1)} collective-permute-done((bf16[256,1024]{1,0:T(8,128)(2,1)S(1)}, bf16[256,1024]{1,0:T(8,128)(2,1)S(1)}, u32[]{:S(2)}, u32[]{:S(2)}) %collective-permute-start.4) | collective-permute-done | bytes 524320 | tf_op jit(solution)/shard_map/ppermute | solution.py:25
  39.4 0.0 collective-permute-start.5
  39.4 0.0 collective-permute-done.8.refs_5_
  39.4 7.2 %collective-permute-start.10 = (bf16[56,4096]{1,0:T(8,128)(2,1)S(1)}, bf16[56,4096]{1,0:T(8,128)(2,1)S(1)}, u32[]{:S(2)}, u32[]{:S(2)}) collective-permute-start(bf16[56,4096]{1,0:T(8,128)(2,1)S(1)} %collective-permute-done.8.refs_5_), channel_id=1, source_target_pairs={{0,255},{1,0},{2,1},{3,2},{4,3},{5,4},{6,5},{7,6},{8,7},{9,8},{10,... | collective-permute-start | bytes 1376264 | tf_op jit(solution)/shard_map/ppermute | solution.py:30
  46.6 0.0 copy-done.6
  46.6 0.0 copy-start.1
  46.6 0.0 copy-start.4
  46.6 4.1 %attend_2.1 = (f32[8,8,256]{2,1,0:T(8,128)S(1)}, f32[8,512,256]{2,1,0:T(8,128)S(1)}) custom-call(bf16[256,4096]{1,0:T(8,128)(2,1)S(1)} %copy-done, bf16[256,1024]{1,0:T(8,128)(2,1)S(1)} %collective-permute-done.1.refs_1_, bf16[256,1024]{1,0:T(8,128)(2,1)S(1)} %collective-permute-done.4.refs_2_, s32[1,256]{1,0:T(1,128)S(1)} %bitcast.5, ...), custom_call_target="tpu_custom_call" | custom-call | flops 1073741824 | bytes 12582912 | tf_op jit(solution)/shard_map/attend_2/pallas_call | solution.py:122
  50.7 0.0 collective-permute-done.9.refs_6_
  50.7 0.1 collective-permute-start.11
  50.8 0.0 collective-permute-done.13.refs_4_
  50.8 1.1 %collective-permute-start.14 = (bf16[56,4096]{1,0:T(8,128)(2,1)S(1)}, bf16[56,4096]{1,0:T(8,128)(2,1)S(1)}, u32[]{:S(2)}, u32[]{:S(2)}) collective-permute-start(bf16[56,4096]{1,0:T(8,128)(2,1)S(1)} %collective-permute-done.13.refs_4_), channel_id=1, source_target_pairs={{0,255},{1,0},{2,1},{3,2},{4,3},{5,4},{6,5},{7,6},{8,7},{9,8},{10,... | collective-permute-start | bytes 1376264 | tf_op jit(solution)/shard_map/ppermute | solution.py:30
  52.0 0.0 collective-permute-done.3.refs_1_
  52.0 1.5 %collective-permute-done.5.refs_2_ = bf16[256,1024]{1,0:T(8,128)(2,1)S(1)} collective-permute-done((bf16[256,1024]{1,0:T(8,128)(2,1)S(1)}, bf16[256,1024]{1,0:T(8,128)(2,1)S(1)}, u32[]{:S(2)}, u32[]{:S(2)}) %collective-permute-start.5) | collective-permute-done | bytes 524320 | tf_op jit(solution)/shard_map/ppermute | solution.py:25
  53.4 0.0 copy-done.1
  53.4 0.0 copy-done.4
  53.4 7.0 %attend_3.1 = (bf16[256,4096]{1,0:T(8,128)(2,1)}, bf16[256,4096]{1,0:T(8,128)(2,1)S(1)}) custom-call(bf16[256,4096]{1,0:T(8,128)(2,1)S(1)} %copy-done, bf16[256,1024]{1,0:T(8,128)(2,1)S(1)} %collective-permute-done.3.refs_1_, bf16[256,1024]{1,0:T(8,128)(2,1)S(1)} %collective-permute-done.5.refs_2_, s32[1,256]{1,0:T(1,128)S(1)} %bitcast.6, ...), custom_call_target="tpu_custom_call" | custom-call | flops 1073741824 | bytes 12582912 | tf_op jit(solution)/shard_map/attend_3/pallas_call | solution.py:122
  60.4 0.0 copy-start.2
  60.4 0.0 copy-start.3
  60.4 0.0 collective-permute-done.10.refs_1_
  60.4 0.0 collective-permute-done.11.refs_2_
  60.4 0.8 %gate_up_1.1.refs_1_ = bf16[64,256]{1,0:T(8,128)(2,1)S(1)} custom-call(bf16[256,4096]{1,0:T(8,128)(2,1)S(1)} %get-tuple-element.31.refs_0_, bf16[56,4096]{1,0:T(8,128)(2,1)S(1)} %collective-permute-done.10.refs_1_, bf16[56,4096]{1,0:T(8,128)(2,1)S(1)} %collective-permute-done.11.refs_2_), custom_call_target="tpu_custom_call" | custom-call | flops 234881024 | bytes 3014656 | tf_op jit(solution)/shard_map/gate_up_1/pallas_call | solution.py:191
  61.3 0.1 copy-done.2
  61.4 0.1 copy-done.3
  61.6 0.0 copy-start.9
  61.6 1.0 %gate_up_3.1.refs_0_ = bf16[192,256]{1,0:T(8,128)(2,1)S(1)} custom-call(bf16[256,4096]{1,0:T(8,128)(2,1)S(1)} %get-tuple-element.31.refs_0_, bf16[56,4096]{1,0:T(8,128)(2,1)S(1)} %copy-done.2, bf16[56,4096]{1,0:T(8,128)(2,1)S(1)} %copy-done.3, bf16[56,4096]{1,0:T(8,128)(2,1)S(1)} %collective-permute-done.6.refs_3_, ...), custom_call_target="tpu_custom_call" | custom-call | flops 704643072 | bytes 4849664 | tf_op jit(solution)/shard_map/gate_up_3/pallas_call | solution.py:191
  62.6 0.0 collective-permute-done.14.refs_5_
  62.6 0.0 copy-done.9
  62.6 1.6 %down.1 = bf16[256,4096]{1,0:T(8,128)(2,1)} custom-call(bf16[192,256]{1,0:T(8,128)(2,1)S(1)} %gate_up_3.1.refs_0_, bf16[64,256]{1,0:T(8,128)(2,1)S(1)} %gate_up_1.1.refs_1_, bf16[56,4096]{1,0:T(8,128)(2,1)S(1)} %copy-done.9, bf16[56,4096]{1,0:T(8,128)(2,1)S(1)} %collective-permute-done.12.refs_3_, bf16[56,4096]{1,0:T(8,128)(2,1)S(1)} %collective-permute-done.13.refs_4_, ...), custom_call_target="tpu_custom_call" | custom-call | flops 30064771072 | bytes 4194304 | tf_op jit(solution)/shard_map/down/pallas_call | solution.py:209
Async XLA Ops:
  0.6 19.0 %collective-permute-start = (bf16[256,1024]{1,0:T(8,128)(2,1)}, bf16[256,1024]{1,0:T(8,128)(2,1)S(1)}, u32[]{:S(2)}, u32[]{:S(2)}) collective-permute-start(bf16[256,1024]{1,0:T(8,128)(2,1)} %refs_1_.2), channel_id=1, source_target_pairs={{0,1},{1,2},{2,3},{3,4},{4,5},{5,6},{6,7},{7,8},{8,9},{9,10},{10,1... | collective-permute-start | bytes 1572872 | tf_op jit(solution)/shard_map/ppermute | solution.py:25
  0.7 20.9 %collective-permute-start.2 = (bf16[256,1024]{1,0:T(8,128)(2,1)}, bf16[256,1024]{1,0:T(8,128)(2,1)S(1)}, u32[]{:S(2)}, u32[]{:S(2)}) collective-permute-start(bf16[256,1024]{1,0:T(8,128)(2,1)} %refs_2_.3), channel_id=1, source_target_pairs={{0,1},{1,2},{2,3},{3,4},{4,5},{5,6},{6,7},{7,8},{8,9},{9,10},{10,1... | collective-permute-start | bytes 1572872 | tf_op jit(solution)/shard_map/ppermute | solution.py:25
  0.8 20.8 %collective-permute-start.6 = (bf16[56,4096]{1,0:T(8,128)(2,1)}, bf16[56,4096]{1,0:T(8,128)(2,1)S(1)}, u32[]{:S(2)}, u32[]{:S(2)}) collective-permute-start(bf16[56,4096]{1,0:T(8,128)(2,1)} %refs_1_.3), channel_id=1, source_target_pairs={{0,255},{1,0},{2,1},{3,2},{4,3},{5,4},{6,5},{7,6},{8,7},{9,8},{10,... | collective-permute-start | bytes 1376264 | tf_op jit(solution)/shard_map/ppermute | solution.py:30
  9.1 19.7 %collective-permute-start.7 = (bf16[56,4096]{1,0:T(8,128)(2,1)}, bf16[56,4096]{1,0:T(8,128)(2,1)S(1)}, u32[]{:S(2)}, u32[]{:S(2)}) collective-permute-start(bf16[56,4096]{1,0:T(8,128)(2,1)} %refs_2_.4), channel_id=1, source_target_pairs={{0,255},{1,0},{2,1},{3,2},{4,3},{5,4},{6,5},{7,6},{8,7},{9,8},{10,... | collective-permute-start | bytes 1376264 | tf_op jit(solution)/shard_map/ppermute | solution.py:30
  9.8 23.2 %collective-permute-start.12 = (bf16[56,4096]{1,0:T(8,128)(2,1)}, bf16[56,4096]{1,0:T(8,128)(2,1)S(1)}, u32[]{:S(2)}, u32[]{:S(2)}) collective-permute-start(bf16[56,4096]{1,0:T(8,128)(2,1)} %refs_2_.5), channel_id=1, source_target_pairs={{0,255},{1,0},{2,1},{3,2},{4,3},{5,4},{6,5},{7,6},{8,7},{9,8},{10,... | collective-permute-start | bytes 1376264 | tf_op jit(solution)/shard_map/ppermute | solution.py:30
  11.4 1.6 %copy-start = (bf16[256,4096]{1,0:T(8,128)(2,1)S(1)}, bf16[256,4096]{1,0:T(8,128)(2,1)}, u32[]{:S(2)}) copy-start(bf16[256,4096]{1,0:T(8,128)(2,1)} %refs_0_.7) | copy-start | bytes 6291460
  13.0 0.7 %copy-start.5 = (s32[256]{0:T(256)S(1)}, s32[256]{0:T(256)}, u32[]{:S(2)}) copy-start(s32[256]{0:T(256)} %param.12) | copy-start | bytes 3076
  13.7 1.0 %copy-start.7 = (bf16[256,1024]{1,0:T(8,128)(2,1)S(1)}, bf16[256,1024]{1,0:T(8,128)(2,1)}, u32[]{:S(2)}) copy-start(bf16[256,1024]{1,0:T(8,128)(2,1)} %refs_1_.2) | copy-start | bytes 1572868
  14.7 1.0 %copy-start.8 = (bf16[256,1024]{1,0:T(8,128)(2,1)S(1)}, bf16[256,1024]{1,0:T(8,128)(2,1)}, u32[]{:S(2)}) copy-start(bf16[256,1024]{1,0:T(8,128)(2,1)} %refs_2_.3) | copy-start | bytes 1572868
  19.6 14.1 %collective-permute-start.1 = (bf16[256,1024]{1,0:T(8,128)(2,1)S(1)}, bf16[256,1024]{1,0:T(8,128)(2,1)S(1)}, u32[]{:S(2)}, u32[]{:S(2)}) collective-permute-start(bf16[256,1024]{1,0:T(8,128)(2,1)S(1)} %collective-permute-done.refs_1_), channel_id=1, source_target_pairs={{0,1},{1,2},{2,3},{3,4},{4,5},{5,6},{6,7},{7,8},{8,9},{9,10},{10,1... | collective-permute-start | bytes 1572872 | tf_op jit(solution)/shard_map/ppermute | solution.py:25
  21.6 17.8 %collective-permute-start.4 = (bf16[256,1024]{1,0:T(8,128)(2,1)S(1)}, bf16[256,1024]{1,0:T(8,128)(2,1)S(1)}, u32[]{:S(2)}, u32[]{:S(2)}) collective-permute-start(bf16[256,1024]{1,0:T(8,128)(2,1)S(1)} %collective-permute-done.2.refs_2_), channel_id=1, source_target_pairs={{0,1},{1,2},{2,3},{3,4},{4,5},{5,6},{6,7},{7,8},{8,9},{9,10},{10,1... | collective-permute-start | bytes 1572872 | tf_op jit(solution)/shard_map/ppermute | solution.py:25
  21.6 17.8 %collective-permute-start.8 = (bf16[56,4096]{1,0:T(8,128)(2,1)S(1)}, bf16[56,4096]{1,0:T(8,128)(2,1)S(1)}, u32[]{:S(2)}, u32[]{:S(2)}) collective-permute-start(bf16[56,4096]{1,0:T(8,128)(2,1)S(1)} %collective-permute-done.6.refs_3_), channel_id=1, source_target_pairs={{0,255},{1,0},{2,1},{3,2},{4,3},{5,4},{6,5},{7,6},{8,7},{9,8},{10,... | collective-permute-start | bytes 1376264 | tf_op jit(solution)/shard_map/ppermute | solution.py:30
  28.8 21.9 %collective-permute-start.9 = (bf16[56,4096]{1,0:T(8,128)(2,1)S(1)}, bf16[56,4096]{1,0:T(8,128)(2,1)S(1)}, u32[]{:S(2)}, u32[]{:S(2)}) collective-permute-start(bf16[56,4096]{1,0:T(8,128)(2,1)S(1)} %collective-permute-done.7.refs_4_), channel_id=1, source_target_pairs={{0,255},{1,0},{2,1},{3,2},{4,3},{5,4},{6,5},{7,6},{8,7},{9,8},{10,... | collective-permute-start | bytes 1376264 | tf_op jit(solution)/shard_map/ppermute | solution.py:30
  28.9 17.7 %copy-start.6 = (s32[256]{0:T(256)S(1)}, s32[256]{0:T(256)}, u32[]{:S(2)}) copy-start(s32[256]{0:T(256)} %param.12) | copy-start | bytes 3076
  33.0 17.8 %collective-permute-start.13 = (bf16[56,4096]{1,0:T(8,128)(2,1)S(1)}, bf16[56,4096]{1,0:T(8,128)(2,1)S(1)}, u32[]{:S(2)}, u32[]{:S(2)}) collective-permute-start(bf16[56,4096]{1,0:T(8,128)(2,1)S(1)} %collective-permute-done.12.refs_3_), channel_id=1, source_target_pairs={{0,255},{1,0},{2,1},{3,2},{4,3},{5,4},{6,5},{7,6},{8,7},{9,8},{10,... | collective-permute-start | bytes 1376264 | tf_op jit(solution)/shard_map/ppermute | solution.py:30
  33.8 18.2 %collective-permute-start.3 = (bf16[256,1024]{1,0:T(8,128)(2,1)S(1)}, bf16[256,1024]{1,0:T(8,128)(2,1)S(1)}, u32[]{:S(2)}, u32[]{:S(2)}) collective-permute-start(bf16[256,1024]{1,0:T(8,128)(2,1)S(1)} %collective-permute-done.1.refs_1_), channel_id=1, source_target_pairs={{0,1},{1,2},{2,3},{3,4},{4,5},{5,6},{6,7},{7,8},{8,9},{9,10},{10,1... | collective-permute-start | bytes 1572872 | tf_op jit(solution)/shard_map/ppermute | solution.py:25
  39.4 14.0 %collective-permute-start.5 = (bf16[256,1024]{1,0:T(8,128)(2,1)S(1)}, bf16[256,1024]{1,0:T(8,128)(2,1)S(1)}, u32[]{:S(2)}, u32[]{:S(2)}) collective-permute-start(bf16[256,1024]{1,0:T(8,128)(2,1)S(1)} %collective-permute-done.4.refs_2_), channel_id=1, source_target_pairs={{0,1},{1,2},{2,3},{3,4},{4,5},{5,6},{6,7},{7,8},{8,9},{9,10},{10,1... | collective-permute-start | bytes 1572872 | tf_op jit(solution)/shard_map/ppermute | solution.py:25
  39.4 21.0 %collective-permute-start.10 = (bf16[56,4096]{1,0:T(8,128)(2,1)S(1)}, bf16[56,4096]{1,0:T(8,128)(2,1)S(1)}, u32[]{:S(2)}, u32[]{:S(2)}) collective-permute-start(bf16[56,4096]{1,0:T(8,128)(2,1)S(1)} %collective-permute-done.8.refs_5_), channel_id=1, source_target_pairs={{0,255},{1,0},{2,1},{3,2},{4,3},{5,4},{6,5},{7,6},{8,7},{9,8},{10,... | collective-permute-start | bytes 1376264 | tf_op jit(solution)/shard_map/ppermute | solution.py:30
  46.6 6.9 %copy-start.1 = (bf16[256,4096]{1,0:T(8,128)(2,1)S(1)}, bf16[256,4096]{1,0:T(8,128)(2,1)}, u32[]{:S(2)}) copy-start(bf16[256,4096]{1,0:T(8,128)(2,1)} %refs_6_.1) | copy-start | bytes 6291460
  46.6 6.9 %copy-start.4 = (f32[4096]{0:T(1024)S(1)}, f32[4096]{0:T(1024)}, u32[]{:S(2)}) copy-start(f32[4096]{0:T(1024)} %param.14) | copy-start | bytes 49156
  50.7 9.7 %collective-permute-start.11 = (bf16[56,4096]{1,0:T(8,128)(2,1)S(1)}, bf16[56,4096]{1,0:T(8,128)(2,1)S(1)}, u32[]{:S(2)}, u32[]{:S(2)}) collective-permute-start(bf16[56,4096]{1,0:T(8,128)(2,1)S(1)} %collective-permute-done.9.refs_6_), channel_id=1, source_target_pairs={{0,255},{1,0},{2,1},{3,2},{4,3},{5,4},{6,5},{7,6},{8,7},{9,8},{10,... | collective-permute-start | bytes 1376264 | tf_op jit(solution)/shard_map/ppermute | solution.py:30
  50.8 11.8 %collective-permute-start.14 = (bf16[56,4096]{1,0:T(8,128)(2,1)S(1)}, bf16[56,4096]{1,0:T(8,128)(2,1)S(1)}, u32[]{:S(2)}, u32[]{:S(2)}) collective-permute-start(bf16[56,4096]{1,0:T(8,128)(2,1)S(1)} %collective-permute-done.13.refs_4_), channel_id=1, source_target_pairs={{0,255},{1,0},{2,1},{3,2},{4,3},{5,4},{6,5},{7,6},{8,7},{9,8},{10,... | collective-permute-start | bytes 1376264 | tf_op jit(solution)/shard_map/ppermute | solution.py:30
  60.4 1.0 %copy-start.2 = (bf16[56,4096]{1,0:T(8,128)(2,1)S(1)}, bf16[56,4096]{1,0:T(8,128)(2,1)}, u32[]{:S(2)}) copy-start(bf16[56,4096]{1,0:T(8,128)(2,1)} %refs_1_.3) | copy-start | bytes 1376260
  60.4 1.1 %copy-start.3 = (bf16[56,4096]{1,0:T(8,128)(2,1)S(1)}, bf16[56,4096]{1,0:T(8,128)(2,1)}, u32[]{:S(2)}) copy-start(bf16[56,4096]{1,0:T(8,128)(2,1)} %refs_2_.4) | copy-start | bytes 1376260
  61.6 1.0 %copy-start.9 = (bf16[56,4096]{1,0:T(8,128)(2,1)S(1)}, bf16[56,4096]{1,0:T(8,128)(2,1)}, u32[]{:S(2)}) copy-start(bf16[56,4096]{1,0:T(8,128)(2,1)} %refs_2_.5) | copy-start | bytes 1376260

commit v3 on v2

--- a/solution.py
+++ b/solution.py
@@ -17,6 +17,7 @@
 UNSEEN = -1e30
 EXPONENT = math.log2(math.e) / math.sqrt(HEAD_SIZE)
 LANES = 128
+CAUSAL_FLOPS = 20 * 10**9
 NT = (((1,), (1,)), ((), ()))
 
 
@@ -36,8 +37,8 @@
 
 def attend_kernel(back, last, *refs):
     if back == 0:
-        q_ref, k_ref, v_ref, position_ref = refs[:4]
-        *out, bias_ref = refs[4:]
+        q_ref, k_ref, v_ref, position_ref, causal_ref = refs[:5]
+        *out, bias_ref = refs[5:]
     else:
         q_ref, k_ref, v_ref, position_ref, stat_ref, sum_ref = refs[:6]
         if last:
@@ -54,9 +55,7 @@
     key = lax.broadcasted_iota(jnp.int32, (rows, rows), 0) - back * rows
     query = lax.broadcasted_iota(jnp.int32, (rows, rows), 1)
     seen = key >= query - position_ref[...]
-    if back == 0:
-        seen = seen & (key <= query)
-    bias_ref[...] = jnp.where(seen, 0.0, UNSEEN)
+    bias_ref[...] = jnp.where(seen, causal_ref[...] if back == 0 else 0.0, UNSEEN)
 
     def group(index, _):
         group_columns = pl.ds(pl.multiple_of(index * HEAD_SIZE, HEAD_SIZE), HEAD_SIZE)
@@ -135,6 +134,120 @@
     )(queries, keys, values, positions, *carry)
 
 
+def weigh_kernel(back, q_ref, k_ref, position_ref, stat_ref, weights_out, stat_out, bias_ref):
+    rows = q_ref.shape[0]
+    key = lax.broadcasted_iota(jnp.int32, (rows, rows), 0) - back * rows
+    query = lax.broadcasted_iota(jnp.int32, (rows, rows), 1)
+    bias_ref[...] = jnp.where(key >= query - position_ref[...], 0.0, UNSEEN)
+
+    def group(index, _):
+        keys = k_ref[:, pl.ds(pl.multiple_of(index * HEAD_SIZE, HEAD_SIZE), HEAD_SIZE)]
+        for head in range(GROUP):
+            columns = pl.ds(pl.multiple_of((index * GROUP + head) * HEAD_SIZE, HEAD_SIZE), HEAD_SIZE)
+            for start in range(0, rows, LANES):
+                some = slice(start, start + LANES)
+                scores = lax.dot_general(
+                    keys, q_ref[some, columns], NT, preferred_element_type=jnp.float32
+                )
+                scores = scores + bias_ref[:, some]
+                top_before = stat_ref[index, head : head + 1, some]
+                top = jnp.maximum(jnp.max(scores, axis=0, keepdims=True), top_before)
+                weights = jnp.exp2((scores - top) * EXPONENT)
+                shrink = jnp.exp2((top_before - top) * EXPONENT)
+                total = jnp.sum(weights, axis=0, keepdims=True)
+                total = total + stat_ref[index, GROUP + head : GROUP + head + 1, some] * shrink
+                weights_out[index, head * rows : (head + 1) * rows, some] = weights.astype(jnp.bfloat16)
+                stat_out[index, head : head + 1, some] = shrink / total
+                stat_out[index, GROUP + head : GROUP + head + 1, some] = 1.0 / total
+        return 0
+
+    lax.fori_loop(0, KEY_VALUE_HEADS, group, 0, unroll=4)
+
+
+def weigh(back, queries, keys, positions, stat):
+    rows = queries.shape[0]
+    return pl.pallas_call(
+        functools.partial(weigh_kernel, back),
+        out_shape=(
+            jax.ShapeDtypeStruct((KEY_VALUE_HEADS, GROUP * rows, rows), jnp.bfloat16),
+            jax.ShapeDtypeStruct(stat.shape, jnp.float32),
+        ),
+        scratch_shapes=[pltpu.VMEM((rows, rows), jnp.float32)],
+        name=f"weigh_{back}",
+        compiler_params=pltpu.CompilerParams(vmem_limit_bytes=16 << 20),
+        cost_estimate=pl.CostEstimate(
+            flops=2 * QUERY_HEADS * rows * rows * HEAD_SIZE,
+            transcendentals=QUERY_HEADS * rows * rows,
+            bytes_accessed=8 << 20,
+        ),
+    )(queries, keys, positions, stat)
+
+
+def mix_kernel(v_ref, weights_ref, stat_ref, sum_ref, residual_ref, gain_ref, attended_out, normed_ref, attended_ref, semaphores):
+    rows = v_ref.shape[0]
+    wide = GROUP * HEAD_SIZE
+
+    def attended_copy(index):
+        columns = pl.ds(pl.multiple_of(index * wide, wide), wide)
+        return pltpu.make_async_copy(attended_ref.at[:, columns], attended_out.at[:, columns], semaphores.at[index])
+
+    def group(index, _):
+        values = v_ref[:, pl.ds(pl.multiple_of(index * HEAD_SIZE, HEAD_SIZE), HEAD_SIZE)].T
+        for head in range(GROUP):
+            columns = pl.ds(pl.multiple_of((index * GROUP + head) * HEAD_SIZE, HEAD_SIZE), HEAD_SIZE)
+            features = slice(head * HEAD_SIZE, (head + 1) * HEAD_SIZE)
+            for start in range(0, rows, LANES):
+                some = slice(start, start + LANES)
+                mixed = jnp.dot(
+                    values,
+                    weights_ref[index, head * rows : (head + 1) * rows, some],
+                    preferred_element_type=jnp.float32,
+                )
+                mixed = mixed * stat_ref[index, GROUP + head : GROUP + head + 1, some]
+                mixed = mixed + sum_ref[index, features, some] * stat_ref[index, head : head + 1, some]
+                attended_ref[some, columns] = mixed.T.astype(jnp.bfloat16)
+        attended_copy(index).start()
+        return 0
+
+    lax.fori_loop(0, KEY_VALUE_HEADS, group, 0, unroll=4)
+    normed_rows(attended_ref, residual_ref, gain_ref, normed_ref)
+    for index in range(KEY_VALUE_HEADS):
+        attended_copy(index).wait()
+
+
+def mix(values, weights, stat, sums, residual, gain):
+    return pl.pallas_call(
+        mix_kernel,
+        out_shape=(jax.ShapeDtypeStruct(residual.shape, jnp.bfloat16),) * 2,
+        out_specs=(pl.BlockSpec(memory_space=pltpu.HBM), pl.BlockSpec(memory_space=pltpu.VMEM)),
+        scratch_shapes=[
+            pltpu.VMEM(residual.shape, jnp.bfloat16),
+            pltpu.SemaphoreType.DMA((KEY_VALUE_HEADS,)),
+        ],
+        name="mix",
+        compiler_params=pltpu.CompilerParams(vmem_limit_bytes=16 << 20),
+        cost_estimate=pl.CostEstimate(
+            flops=2 * weights.size * HEAD_SIZE, transcendentals=0, bytes_accessed=12 << 20
+        ),
+    )(values, weights, stat, sums, residual, gain)
+
+
+def causal_kernel(out_ref):
+    key = lax.broadcasted_iota(jnp.int32, out_ref.shape, 0)
+    query = lax.broadcasted_iota(jnp.int32, out_ref.shape, 1)
+    out_ref[...] = jnp.where(key <= query, 0.0, UNSEEN)
+
+
+def causal_bias(rows):
+    return pl.pallas_call(
+        causal_kernel,
+        out_shape=jax.ShapeDtypeStruct((rows, rows), jnp.float32),
+        name="causal",
+        compiler_params=pltpu.CompilerParams(vmem_limit_bytes=4 << 20),
+        cost_estimate=pl.CostEstimate(flops=CAUSAL_FLOPS, transcendentals=0, bytes_accessed=rows * rows * 4),
+    )()
+
+
 def normed_rows(attended_ref, residual_ref, gain_ref, out_ref):
     step = 16
 
@@ -164,14 +277,14 @@
 
 
 def down_kernel(slot, *refs):
-    early_ref, late_ref = refs[:2]
-    downs = refs[2 : 2 + FFN_STEPS]
-    out_ref, rhs_ref, piece_ref, semaphores = refs[2 + FFN_STEPS :]
+    hidden_ref = refs[0]
+    downs = refs[1 : 1 + FFN_STEPS]
+    out_ref, rhs_ref, piece_ref, semaphores = refs[1 + FFN_STEPS :]
     units = downs[0].shape[0]
     for index, rows in enumerate(downs):
         rhs_ref[index * slot : index * slot + units, :] = rows[...]
         rhs_ref[index * slot + units : (index + 1) * slot, :] = jnp.zeros((slot - units, rhs_ref.shape[1]), rhs_ref.dtype)
-    hidden = jnp.concatenate([early_ref[...], late_ref[...]], axis=0).T
+    hidden = hidden_ref[...].T
     width = out_ref.shape[1] // semaphores.shape[0]
     copies = []
     for piece in range(semaphores.shape[0]):
@@ -202,10 +315,10 @@
     )(normed, *weights)
 
 
-def down(early, late, downs):
+def down(hidden, downs):
     units, features = downs[0].shape
-    rows = early.shape[1]
-    slot = late.shape[0]
+    rows = hidden.shape[1]
+    slot = hidden.shape[0] // FFN_STEPS
     return pl.pallas_call(
         functools.partial(down_kernel, slot),
         out_shape=jax.ShapeDtypeStruct((rows, features), jnp.bfloat16),
@@ -222,7 +335,7 @@
             transcendentals=0,
             bytes_accessed=4 << 20,
         ),
-    )(early, late, *downs)
+    )(hidden, *downs)
 
 
 def per_device(
@@ -240,13 +353,14 @@
     keys = [rotated_key_state]
     values = [value_state_rows]
     gates, ups, downs = [gate_weight], [up_weight], [down_weight]
-    gates.append(to_previous(gates[0]))
-    ups.append(to_previous(ups[0]))
-    downs.append(to_previous(downs[0]))
-    keys.append(to_next(keys[0]))
-    values.append(to_next(values[0]))
-
-    carry = attend(0, False, query_states, keys[0], values[0], positions)
+    causal = causal_bias(query_states.shape[0])
+    gates.append(to_previous(after(gates[0], causal)))
+    ups.append(to_previous(after(ups[0], causal)))
+    downs.append(to_previous(after(downs[0], causal)))
+    keys.append(to_next(after(keys[0], causal)))
+    values.append(to_next(after(values[0], causal)))
+
+    carry = attend(0, False, query_states, keys[0], values[0], positions, (causal,))
     keys.append(to_next(after(keys[1], carry[0])))
     gates.append(to_previous(after(gates[1], carry[0])))
     values.append(to_next(after(values[1], carry[0])))
@@ -262,12 +376,10 @@
     ups.append(to_previous(after(ups[2], carry[0])))
     downs.append(to_previous(after(downs[2], carry[0])))
 
-    attended, normed = attend(
-        3, True, query_states, keys[3], values[3], positions, (*carry, residual, norm_gain[None, :])
-    )
-    early = gate_up(normed, gates[0], ups[0], gates[1], ups[1], gates[2], ups[2])
-    late = gate_up(normed, gates[3], ups[3])
-    ffn_part = down(early, late, downs)
+    weights, scales = weigh(3, query_states, keys[3], positions, carry[0])
+    attended, normed = mix(values[3], weights, scales, carry[1], residual, norm_gain[None, :])
+    units = gate_up(normed, *[rows for pair in zip(gates, ups) for rows in pair])
+    ffn_part = down(units, downs)
     return (attended, ffn_part)
 
 

time: 65.4 us -> 63 us (0.963); the launches traced: 64.4 us -> 62.9 us
  starting transfers between devices: 26.6 us -> 30.5 us
  local copies, waits for them, and re-layouts: 4.65 us -> 1.27 us
  waiting for transfers between devices: 9.6 us -> 8.16 us
    pallas_call x0 -> x3, Pallas kernels: none -> 7.08 us  [the longest x1 3.61 us: mix(): pl.pallas_call(mix_kernel, out_shape=(jax.ShapeDtypeStruct(residual.shape...]
    pallas_call x4 -> x3, Pallas kernels: 19.1 us -> 12 us  [attend(): pl.pallas_call(functools.partial(attend_kernel, back, last), out_shape=ou...]
    ppermute x9, starting transfers between devices: 26.4 us -> 30 us  [to_previous(): lax.ppermute(value, 'blk', [(i, (i - 1) % count) for i in range(count)])]
    unnamed x20 -> x18, local copies, waits for them, and re-layouts: 4.65 us -> 1.27 us
    ppermute x6, waiting for transfers between devices: 9.58 us -> 8.13 us  [to_next(): lax.ppermute(value, 'blk', [(i, (i + 1) % count) for i in range(count)])]
    pallas_call x2 -> x1, Pallas kernels: 1.84 us -> 1.3 us  [gate_up(): pl.pallas_call(functools.partial(gate_kernel, shards, slot), out_shape=ja...]
  transfers between devices with their start and end apart: 15 -> 15, of which waited for: 4 -> 3; matrix products, arithmetic and copies ran while one was open for 0% -> 0% of each run, Pallas kernels for 32% -> 32%
where the time goes in v3:
time: 63 us; the launch traced here: 62.9 us
  starting transfers between devices  30.5 us (48%)
  Pallas kernels  22 us (35%)
  waiting for transfers between devices  8.16 us (13%)
  local copies, waits for them, and re-layouts  1.27 us (2%)
  between operations  1.01 us (2%)
    ppermute x9, starting transfers between devices, to_previous(): lax.ppermute(value, 'blk', [(i, (i - 1) % count) for i in range(count)])  30 us
    pallas_call x3, Pallas kernels, attend(): pl.pallas_call(functools.partial(attend_kernel, back, last), out_shape=ou...  12 us
    ppermute x6, waiting for transfers between devices, to_next(): lax.ppermute(value, 'blk', [(i, (i + 1) % count) for i in range(count)])  8.13 us
    pallas_call x1, Pallas kernels, mix(): pl.pallas_call(mix_kernel, out_shape=(jax.ShapeDtypeStruct(residual.shape...  3.61 us
    pallas_call x1, Pallas kernels, weigh(): pl.pallas_call(functools.partial(weigh_kernel, back), out_shape=(jax.Shap...  3.45 us
    pallas_call x1, Pallas kernels, down(): pl.pallas_call(functools.partial(down_kernel, slot), out_shape=jax.ShapeD...  1.63 us
    pallas_call x1, Pallas kernels, gate_up(): pl.pallas_call(functools.partial(gate_kernel, shards, slot), out_shape=ja...  1.3 us
    unnamed x18, local copies, waits for them, and re-layouts  1.27 us
  transfers between devices with their start and end apart: 15, of which 3 were waited for; matrix products, arithmetic and copies ran while one was open for 0% of the time, Pallas kernels for 32%

profile of v3, /device:TPU:0, one launch (start us, length us, event | category | flops | bytes accessed | tf_op | source)
XLA Modules:
  0.0 62.9 jit_solution(11826855498782705927)
XLA Ops:
  0.6 0.0 copy-start.6
  0.6 0.0 copy-start.7
  0.7 0.0 copy-start.2
  0.7 0.0 copy-start.3
  0.7 0.0 copy-start.8
  0.7 0.0 copy-start
  0.7 0.0 copy-start.5
  0.7 0.9 %copy-done.6 = bf16[256,1024]{1,0:T(8,128)(2,1)S(1)} copy-done((bf16[256,1024]{1,0:T(8,128)(2,1)S(1)}, bf16[256,1024]{1,0:T(8,128)(2,1)}, u32[]{:S(2)}) %copy-start.6) | copy-done | bytes 524312
  1.7 0.0 collective-permute-start.2
  1.7 0.2 copy-done.7
  1.8 0.0 collective-permute-start
  1.8 0.1 copy-done.2
  2.0 8.2 %collective-permute-start.6 = (bf16[56,4096]{1,0:T(8,128)(2,1)S(1)}, bf16[56,4096]{1,0:T(8,128)(2,1)S(1)}, u32[]{:S(2)}, u32[]{:S(2)}) collective-permute-start(bf16[56,4096]{1,0:T(8,128)(2,1)S(1)} %copy-done.2), channel_id=1, source_target_pairs={{0,255},{1,0},{2,1},{3,2},{4,3},{5,4},{6,5},{7,6},{8,7},{9,8},{10,... | collective-permute-start | bytes 1376264 | tf_op jit(solution)/shard_map/ppermute | solution.py:31
  10.2 0.0 copy-done.3
  10.2 0.7 %collective-permute-start.7 = (bf16[56,4096]{1,0:T(8,128)(2,1)S(1)}, bf16[56,4096]{1,0:T(8,128)(2,1)S(1)}, u32[]{:S(2)}, u32[]{:S(2)}) collective-permute-start(bf16[56,4096]{1,0:T(8,128)(2,1)S(1)} %copy-done.3), channel_id=1, source_target_pairs={{0,255},{1,0},{2,1},{3,2},{4,3},{5,4},{6,5},{7,6},{8,7},{9,8},{10,... | collective-permute-start | bytes 1376264 | tf_op jit(solution)/shard_map/ppermute | solution.py:31
  10.9 0.0 copy-done.8
  10.9 1.6 %collective-permute-start.12 = (bf16[56,4096]{1,0:T(8,128)(2,1)S(1)}, bf16[56,4096]{1,0:T(8,128)(2,1)S(1)}, u32[]{:S(2)}, u32[]{:S(2)}) collective-permute-start(bf16[56,4096]{1,0:T(8,128)(2,1)S(1)} %copy-done.8), channel_id=1, source_target_pairs={{0,255},{1,0},{2,1},{3,2},{4,3},{5,4},{6,5},{7,6},{8,7},{9,8},{10,... | collective-permute-start | bytes 1376264 | tf_op jit(solution)/shard_map/ppermute | solution.py:31
  12.5 0.0 copy-done
  12.5 0.0 copy-done.5
  12.5 3.8 %attend_0.1 = (f32[8,8,256]{2,1,0:T(8,128)S(1)}, f32[8,512,256]{2,1,0:T(8,128)S(1)}) custom-call(bf16[256,4096]{1,0:T(8,128)(2,1)S(1)} %copy-done, bf16[256,1024]{1,0:T(8,128)(2,1)S(1)} %copy-done.6, bf16[256,1024]{1,0:T(8,128)(2,1)S(1)} %copy-done.7, s32[1,256]{1,0:T(1,128)S(1)} %bitcast.3, f32[256,256]{1,0:T(8,128)S(1)} %causal.1.refs_4_), custom_call_target="tpu_custom_call" | custom-call | flops 1073741824 | bytes 12582912 | tf_op jit(solution)/shard_map/attend_0/pallas_call | solution.py:121
  16.3 0.5 collective-permute-done.2.refs_1_
  16.7 0.0 collective-permute-start.4
  16.7 5.6 %collective-permute-done.refs_2_ = bf16[256,1024]{1,0:T(8,128)(2,1)S(1)} collective-permute-done((bf16[256,1024]{1,0:T(8,128)(2,1)S(1)}, bf16[256,1024]{1,0:T(8,128)(2,1)S(1)}, u32[]{:S(2)}, u32[]{:S(2)}) %collective-permute-start) | collective-permute-done | bytes 524320 | tf_op jit(solution)/shard_map/ppermute | solution.py:26
  22.4 0.0 collective-permute-start.1
  22.4 0.0 collective-permute-done.6.refs_3_
  22.4 7.2 %collective-permute-start.8 = (bf16[56,4096]{1,0:T(8,128)(2,1)S(1)}, bf16[56,4096]{1,0:T(8,128)(2,1)S(1)}, u32[]{:S(2)}, u32[]{:S(2)}) collective-permute-start(bf16[56,4096]{1,0:T(8,128)(2,1)S(1)} %collective-permute-done.6.refs_3_), channel_id=1, source_target_pairs={{0,255},{1,0},{2,1},{3,2},{4,3},{5,4},{6,5},{7,6},{8,7},{9,8},{10,... | collective-permute-start | bytes 1376264 | tf_op jit(solution)/shard_map/ppermute | solution.py:31
  29.5 0.0 collective-permute-done.7.refs_4_
  29.5 0.1 collective-permute-start.9
  29.6 4.1 %attend_1.1 = (f32[8,8,256]{2,1,0:T(8,128)S(1)}, f32[8,512,256]{2,1,0:T(8,128)S(1)}) custom-call(bf16[256,4096]{1,0:T(8,128)(2,1)S(1)} %copy-done, bf16[256,1024]{1,0:T(8,128)(2,1)S(1)} %collective-permute-done.2.refs_1_, bf16[256,1024]{1,0:T(8,128)(2,1)S(1)} %collective-permute-done.refs_2_, s32[1,256]{1,0:T(1,128)S(1)} %bitcast.4, ...), custom_call_target="tpu_custom_call" | custom-call | flops 1073741824 | bytes 12582912 | tf_op jit(solution)/shard_map/attend_1/pallas_call | solution.py:121
  33.7 0.0 collective-permute-done.12.refs_2_
  33.7 0.1 collective-permute-start.13
  33.8 0.0 collective-permute-done.4.refs_1_
  33.8 0.5 collective-permute-start.5
  34.4 2.0 %collective-permute-done.1.refs_2_ = bf16[256,1024]{1,0:T(8,128)(2,1)S(1)} collective-permute-done((bf16[256,1024]{1,0:T(8,128)(2,1)S(1)}, bf16[256,1024]{1,0:T(8,128)(2,1)S(1)}, u32[]{:S(2)}, u32[]{:S(2)}) %collective-permute-start.1) | collective-permute-done | bytes 524320 | tf_op jit(solution)/shard_map/ppermute | solution.py:26
  36.4 0.0 collective-permute-start.3
  36.4 0.0 collective-permute-done.8.refs_5_
  36.4 7.2 %collective-permute-start.10 = (bf16[56,4096]{1,0:T(8,128)(2,1)S(1)}, bf16[56,4096]{1,0:T(8,128)(2,1)S(1)}, u32[]{:S(2)}, u32[]{:S(2)}) collective-permute-start(bf16[56,4096]{1,0:T(8,128)(2,1)S(1)} %collective-permute-done.8.refs_5_), channel_id=1, source_target_pairs={{0,255},{1,0},{2,1},{3,2},{4,3},{5,4},{6,5},{7,6},{8,7},{9,8},{10,... | collective-permute-start | bytes 1376264 | tf_op jit(solution)/shard_map/ppermute | solution.py:31
  43.6 4.1 %attend_2.1 = (f32[8,8,256]{2,1,0:T(8,128)S(1)}, f32[8,512,256]{2,1,0:T(8,128)S(1)}) custom-call(bf16[256,4096]{1,0:T(8,128)(2,1)S(1)} %copy-done, bf16[256,1024]{1,0:T(8,128)(2,1)S(1)} %collective-permute-done.4.refs_1_, bf16[256,1024]{1,0:T(8,128)(2,1)S(1)} %collective-permute-done.1.refs_2_, s32[1,256]{1,0:T(1,128)S(1)} %bitcast.5, ...), custom_call_target="tpu_custom_call" | custom-call | flops 1073741824 | bytes 12582912 | tf_op jit(solution)/shard_map/attend_2/pallas_call | solution.py:121
  47.7 0.0 copy-start.1
  47.7 0.0 copy-start.4
  47.7 0.0 collective-permute-done.9.refs_6_
  47.7 0.1 collective-permute-start.11
  47.8 0.0 collective-permute-done.13.refs_3_
  47.8 4.9 %collective-permute-start.14 = (bf16[56,4096]{1,0:T(8,128)(2,1)S(1)}, bf16[56,4096]{1,0:T(8,128)(2,1)S(1)}, u32[]{:S(2)}, u32[]{:S(2)}) collective-permute-start(bf16[56,4096]{1,0:T(8,128)(2,1)S(1)} %collective-permute-done.13.refs_3_), channel_id=1, source_target_pairs={{0,255},{1,0},{2,1},{3,2},{4,3},{5,4},{6,5},{7,6},{8,7},{9,8},{10,... | collective-permute-start | bytes 1376264 | tf_op jit(solution)/shard_map/ppermute | solution.py:31
  52.7 0.0 collective-permute-done.5.k_ref
  52.7 3.5 %weigh_3.1 = (bf16[8,1024,256]{2,1,0:T(8,128)(2,1)S(1)}, f32[8,8,256]{2,1,0:T(8,128)S(1)}) custom-call(bf16[256,4096]{1,0:T(8,128)(2,1)S(1)} %copy-done, bf16[256,1024]{1,0:T(8,128)(2,1)S(1)} %collective-permute-done.5.k_ref, s32[1,256]{1,0:T(1,128)S(1)} %bitcast.6, f32[8,8,256]{2,1,0:T(8,128)S(1)} %get-tuple-element.37.stat_ref), custom_call_target="tpu_custom_call" | custom-call | flops 536870912 | bytes 8388608 | tf_op jit(solution)/shard_map/weigh_3/pallas_call | solution.py:169
  56.2 0.0 collective-permute-done.3.v_ref
  56.2 0.0 copy-done.1
  56.2 0.0 copy-done.4
  56.2 3.6 %mix.1 = (bf16[256,4096]{1,0:T(8,128)(2,1)}, bf16[256,4096]{1,0:T(8,128)(2,1)S(1)}) custom-call(bf16[256,1024]{1,0:T(8,128)(2,1)S(1)} %collective-permute-done.3.v_ref, bf16[8,1024,256]{2,1,0:T(8,128)(2,1)S(1)} %get-tuple-element.38.weights_ref, f32[8,8,256]{2,1,0:T(8,128)S(1)} %get-tuple-element.39.stat_ref, f32[8,512,256]{2,1,0:T(8,128)S(1)} %get-tuple-element.40.sum_ref, ...), custom_call_target="tpu_custom_call" | custom-call | flops 536870912 | bytes 12582912 | tf_op jit(solution)/shard_map/mix/pallas_call | solution.py:219
  59.8 0.0 collective-permute-done.10.refs_7_
  59.8 0.0 collective-permute-done.11.refs_8_
  59.8 1.3 %gate_up_4.1.refs_0_ = bf16[256,256]{1,0:T(8,128)(2,1)S(1)} custom-call(bf16[256,4096]{1,0:T(8,128)(2,1)S(1)} %get-tuple-element.42.refs_0_, bf16[56,4096]{1,0:T(8,128)(2,1)S(1)} %copy-done.2, bf16[56,4096]{1,0:T(8,128)(2,1)S(1)} %copy-done.3, bf16[56,4096]{1,0:T(8,128)(2,1)S(1)} %collective-permute-done.6.refs_3_, ...), custom_call_target="tpu_custom_call" | custom-call | flops 939524096 | bytes 5767168 | tf_op jit(solution)/shard_map/gate_up_4/pallas_call | solution.py:304
  61.1 0.0 collective-permute-done.14.refs_4_
  61.1 1.6 %down.1 = bf16[256,4096]{1,0:T(8,128)(2,1)} custom-call(bf16[256,256]{1,0:T(8,128)(2,1)S(1)} %gate_up_4.1.refs_0_, bf16[56,4096]{1,0:T(8,128)(2,1)S(1)} %copy-done.8, bf16[56,4096]{1,0:T(8,128)(2,1)S(1)} %collective-permute-done.12.refs_2_, bf16[56,4096]{1,0:T(8,128)(2,1)S(1)} %collective-permute-done.13.refs_3_, ...), custom_call_target="tpu_custom_call" | custom-call | flops 30064771072 | bytes 4194304 | tf_op jit(solution)/shard_map/down/pallas_call | solution.py:322
  (1 shorter events, 0.0 us)
Async XLA Ops:
  0.6 1.0 %copy-start.6 = (bf16[256,1024]{1,0:T(8,128)(2,1)S(1)}, bf16[256,1024]{1,0:T(8,128)(2,1)}, u32[]{:S(2)}) copy-start(bf16[256,1024]{1,0:T(8,128)(2,1)} %refs_1_.3) | copy-start | bytes 1572868
  0.6 1.2 %copy-start.7 = (bf16[256,1024]{1,0:T(8,128)(2,1)S(1)}, bf16[256,1024]{1,0:T(8,128)(2,1)}, u32[]{:S(2)}) copy-start(bf16[256,1024]{1,0:T(8,128)(2,1)} %refs_2_.2) | copy-start | bytes 1572868
  0.7 1.3 %copy-start.2 = (bf16[56,4096]{1,0:T(8,128)(2,1)S(1)}, bf16[56,4096]{1,0:T(8,128)(2,1)}, u32[]{:S(2)}) copy-start(bf16[56,4096]{1,0:T(8,128)(2,1)} %refs_1_.4) | copy-start | bytes 1376260
  0.7 9.5 %copy-start.3 = (bf16[56,4096]{1,0:T(8,128)(2,1)S(1)}, bf16[56,4096]{1,0:T(8,128)(2,1)}, u32[]{:S(2)}) copy-start(bf16[56,4096]{1,0:T(8,128)(2,1)} %refs_2_.3) | copy-start | bytes 1376260
  0.7 10.2 %copy-start.8 = (bf16[56,4096]{1,0:T(8,128)(2,1)S(1)}, bf16[56,4096]{1,0:T(8,128)(2,1)}, u32[]{:S(2)}) copy-start(bf16[56,4096]{1,0:T(8,128)(2,1)} %refs_1_.5) | copy-start | bytes 1376260
  0.7 11.8 %copy-start = (bf16[256,4096]{1,0:T(8,128)(2,1)S(1)}, bf16[256,4096]{1,0:T(8,128)(2,1)}, u32[]{:S(2)}) copy-start(bf16[256,4096]{1,0:T(8,128)(2,1)} %q_ref.1) | copy-start | bytes 6291460
  0.7 11.8 %copy-start.5 = (s32[256]{0:T(256)S(1)}, s32[256]{0:T(256)}, u32[]{:S(2)}) copy-start(s32[256]{0:T(256)} %param.12) | copy-start | bytes 3076
  1.7 15.1 %collective-permute-start.2 = (bf16[256,1024]{1,0:T(8,128)(2,1)S(1)}, bf16[256,1024]{1,0:T(8,128)(2,1)S(1)}, u32[]{:S(2)}, u32[]{:S(2)}) collective-permute-start(bf16[256,1024]{1,0:T(8,128)(2,1)S(1)} %copy-done.6), channel_id=1, source_target_pairs={{0,1},{1,2},{2,3},{3,4},{4,5},{5,6},{6,7},{7,8},{8,9},{9,10},{10,1... | collective-permute-start | bytes 1572872 | tf_op jit(solution)/shard_map/ppermute | solution.py:26
  1.8 20.5 %collective-permute-start = (bf16[256,1024]{1,0:T(8,128)(2,1)S(1)}, bf16[256,1024]{1,0:T(8,128)(2,1)S(1)}, u32[]{:S(2)}, u32[]{:S(2)}) collective-permute-start(bf16[256,1024]{1,0:T(8,128)(2,1)S(1)} %copy-done.7), channel_id=1, source_target_pairs={{0,1},{1,2},{2,3},{3,4},{4,5},{5,6},{6,7},{7,8},{8,9},{9,10},{10,1... | collective-permute-start | bytes 1572872 | tf_op jit(solution)/shard_map/ppermute | solution.py:26
  2.0 20.4 %collective-permute-start.6 = (bf16[56,4096]{1,0:T(8,128)(2,1)S(1)}, bf16[56,4096]{1,0:T(8,128)(2,1)S(1)}, u32[]{:S(2)}, u32[]{:S(2)}) collective-permute-start(bf16[56,4096]{1,0:T(8,128)(2,1)S(1)} %copy-done.2), channel_id=1, source_target_pairs={{0,255},{1,0},{2,1},{3,2},{4,3},{5,4},{6,5},{7,6},{8,7},{9,8},{10,... | collective-permute-start | bytes 1376264 | tf_op jit(solution)/shard_map/ppermute | solution.py:31
  10.2 19.4 %collective-permute-start.7 = (bf16[56,4096]{1,0:T(8,128)(2,1)S(1)}, bf16[56,4096]{1,0:T(8,128)(2,1)S(1)}, u32[]{:S(2)}, u32[]{:S(2)}) collective-permute-start(bf16[56,4096]{1,0:T(8,128)(2,1)S(1)} %copy-done.3), channel_id=1, source_target_pairs={{0,255},{1,0},{2,1},{3,2},{4,3},{5,4},{6,5},{7,6},{8,7},{9,8},{10,... | collective-permute-start | bytes 1376264 | tf_op jit(solution)/shard_map/ppermute | solution.py:31
  10.9 22.9 %collective-permute-start.12 = (bf16[56,4096]{1,0:T(8,128)(2,1)S(1)}, bf16[56,4096]{1,0:T(8,128)(2,1)S(1)}, u32[]{:S(2)}, u32[]{:S(2)}) collective-permute-start(bf16[56,4096]{1,0:T(8,128)(2,1)S(1)} %copy-done.8), channel_id=1, source_target_pairs={{0,255},{1,0},{2,1},{3,2},{4,3},{5,4},{6,5},{7,6},{8,7},{9,8},{10,... | collective-permute-start | bytes 1376264 | tf_op jit(solution)/shard_map/ppermute | solution.py:31
  16.7 17.1 %collective-permute-start.4 = (bf16[256,1024]{1,0:T(8,128)(2,1)S(1)}, bf16[256,1024]{1,0:T(8,128)(2,1)S(1)}, u32[]{:S(2)}, u32[]{:S(2)}) collective-permute-start(bf16[256,1024]{1,0:T(8,128)(2,1)S(1)} %collective-permute-done.2.refs_1_), channel_id=1, source_target_pairs={{0,1},{1,2},{2,3},{3,4},{4,5},{5,6},{6,7},{7,8},{8,9},{9,10},{10,1... | collective-permute-start | bytes 1572872 | tf_op jit(solution)/shard_map/ppermute | solution.py:26
  22.4 14.0 %collective-permute-start.1 = (bf16[256,1024]{1,0:T(8,128)(2,1)S(1)}, bf16[256,1024]{1,0:T(8,128)(2,1)S(1)}, u32[]{:S(2)}, u32[]{:S(2)}) collective-permute-start(bf16[256,1024]{1,0:T(8,128)(2,1)S(1)} %collective-permute-done.refs_2_), channel_id=1, source_target_pairs={{0,1},{1,2},{2,3},{3,4},{4,5},{5,6},{6,7},{7,8},{8,9},{9,10},{10,1... | collective-permute-start | bytes 1572872 | tf_op jit(solution)/shard_map/ppermute | solution.py:26
  22.4 14.0 %collective-permute-start.8 = (bf16[56,4096]{1,0:T(8,128)(2,1)S(1)}, bf16[56,4096]{1,0:T(8,128)(2,1)S(1)}, u32[]{:S(2)}, u32[]{:S(2)}) collective-permute-start(bf16[56,4096]{1,0:T(8,128)(2,1)S(1)} %collective-permute-done.6.refs_3_), channel_id=1, source_target_pairs={{0,255},{1,0},{2,1},{3,2},{4,3},{5,4},{6,5},{7,6},{8,7},{9,8},{10,... | collective-permute-start | bytes 1376264 | tf_op jit(solution)/shard_map/ppermute | solution.py:31
  29.5 18.2 %collective-permute-start.9 = (bf16[56,4096]{1,0:T(8,128)(2,1)S(1)}, bf16[56,4096]{1,0:T(8,128)(2,1)S(1)}, u32[]{:S(2)}, u32[]{:S(2)}) collective-permute-start(bf16[56,4096]{1,0:T(8,128)(2,1)S(1)} %collective-permute-done.7.refs_4_), channel_id=1, source_target_pairs={{0,255},{1,0},{2,1},{3,2},{4,3},{5,4},{6,5},{7,6},{8,7},{9,8},{10,... | collective-permute-start | bytes 1376264 | tf_op jit(solution)/shard_map/ppermute | solution.py:31
  33.7 14.1 %collective-permute-start.13 = (bf16[56,4096]{1,0:T(8,128)(2,1)S(1)}, bf16[56,4096]{1,0:T(8,128)(2,1)S(1)}, u32[]{:S(2)}, u32[]{:S(2)}) collective-permute-start(bf16[56,4096]{1,0:T(8,128)(2,1)S(1)} %collective-permute-done.12.refs_2_), channel_id=1, source_target_pairs={{0,255},{1,0},{2,1},{3,2},{4,3},{5,4},{6,5},{7,6},{8,7},{9,8},{10,... | collective-permute-start | bytes 1376264 | tf_op jit(solution)/shard_map/ppermute | solution.py:31
  33.8 18.9 %collective-permute-start.5 = (bf16[256,1024]{1,0:T(8,128)(2,1)S(1)}, bf16[256,1024]{1,0:T(8,128)(2,1)S(1)}, u32[]{:S(2)}, u32[]{:S(2)}) collective-permute-start(bf16[256,1024]{1,0:T(8,128)(2,1)S(1)} %collective-permute-done.4.refs_1_), channel_id=1, source_target_pairs={{0,1},{1,2},{2,3},{3,4},{4,5},{5,6},{6,7},{7,8},{8,9},{9,10},{10,1... | collective-permute-start | bytes 1572872 | tf_op jit(solution)/shard_map/ppermute | solution.py:26
  36.4 19.8 %collective-permute-start.3 = (bf16[256,1024]{1,0:T(8,128)(2,1)S(1)}, bf16[256,1024]{1,0:T(8,128)(2,1)S(1)}, u32[]{:S(2)}, u32[]{:S(2)}) collective-permute-start(bf16[256,1024]{1,0:T(8,128)(2,1)S(1)} %collective-permute-done.1.refs_2_), channel_id=1, source_target_pairs={{0,1},{1,2},{2,3},{3,4},{4,5},{5,6},{6,7},{7,8},{8,9},{9,10},{10,1... | collective-permute-start | bytes 1572872 | tf_op jit(solution)/shard_map/ppermute | solution.py:26
  36.4 23.4 %collective-permute-start.10 = (bf16[56,4096]{1,0:T(8,128)(2,1)S(1)}, bf16[56,4096]{1,0:T(8,128)(2,1)S(1)}, u32[]{:S(2)}, u32[]{:S(2)}) collective-permute-start(bf16[56,4096]{1,0:T(8,128)(2,1)S(1)} %collective-permute-done.8.refs_5_), channel_id=1, source_target_pairs={{0,255},{1,0},{2,1},{3,2},{4,3},{5,4},{6,5},{7,6},{8,7},{9,8},{10,... | collective-permute-start | bytes 1376264 | tf_op jit(solution)/shard_map/ppermute | solution.py:31
  47.7 8.5 %copy-start.1 = (bf16[256,4096]{1,0:T(8,128)(2,1)S(1)}, bf16[256,4096]{1,0:T(8,128)(2,1)}, u32[]{:S(2)}) copy-start(bf16[256,4096]{1,0:T(8,128)(2,1)} %residual_ref.1) | copy-start | bytes 6291460
  47.7 8.5 %copy-start.4 = (f32[4096]{0:T(1024)S(1)}, f32[4096]{0:T(1024)}, u32[]{:S(2)}) copy-start(f32[4096]{0:T(1024)} %param.14) | copy-start | bytes 49156
  47.7 12.1 %collective-permute-start.11 = (bf16[56,4096]{1,0:T(8,128)(2,1)S(1)}, bf16[56,4096]{1,0:T(8,128)(2,1)S(1)}, u32[]{:S(2)}, u32[]{:S(2)}) collective-permute-start(bf16[56,4096]{1,0:T(8,128)(2,1)S(1)} %collective-permute-done.9.refs_6_), channel_id=1, source_target_pairs={{0,255},{1,0},{2,1},{3,2},{4,3},{5,4},{6,5},{7,6},{8,7},{9,8},{10,... | collective-permute-start | bytes 1376264 | tf_op jit(solution)/shard_map/ppermute | solution.py:31
  47.8 13.3 %collective-permute-start.14 = (bf16[56,4096]{1,0:T(8,128)(2,1)S(1)}, bf16[56,4096]{1,0:T(8,128)(2,1)S(1)}, u32[]{:S(2)}, u32[]{:S(2)}) collective-permute-start(bf16[56,4096]{1,0:T(8,128)(2,1)S(1)} %collective-permute-done.13.refs_3_), channel_id=1, source_target_pairs={{0,255},{1,0},{2,1},{3,2},{4,3},{5,4},{6,5},{7,6},{8,7},{9,8},{10,... | collective-permute-start | bytes 1376264 | tf_op jit(solution)/shard_map/ppermute | solution.py:31

commit v4 on v3

--- a/solution.py
+++ b/solution.py
@@ -91,7 +91,7 @@
             attended_copy(index).start()
         return 0
 
-    lax.fori_loop(0, KEY_VALUE_HEADS, group, 0, unroll=4)
+    lax.fori_loop(0, KEY_VALUE_HEADS, group, 0, unroll=True)
     if last:
         normed_rows(attended_ref, residual_ref, gain_ref, normed_ref)
         for index in range(KEY_VALUE_HEADS):
@@ -161,7 +161,7 @@
                 stat_out[index, GROUP + head : GROUP + head + 1, some] = 1.0 / total
         return 0
 
-    lax.fori_loop(0, KEY_VALUE_HEADS, group, 0, unroll=4)
+    lax.fori_loop(0, KEY_VALUE_HEADS, group, 0, unroll=True)
 
 
 def weigh(back, queries, keys, positions, stat):

time: 63 us -> 62.9 us (level)
  Pallas kernels: 22 us -> 20.3 us
  waiting for transfers between devices: 8.16 us -> 9.11 us
  starting transfers between devices: 30.5 us -> 31.2 us
    pallas_call x3, Pallas kernels: 12 us -> 10.4 us  [attend(): pl.pallas_call(functools.partial(attend_kernel, back, last), out_shape=ou...]
    ppermute x6, waiting for transfers between devices: 8.13 us -> 9.09 us  [to_next(): lax.ppermute(value, 'blk', [(i, (i + 1) % count) for i in range(count)])]
    ppermute x9, starting transfers between devices: 30 us -> 30.7 us  [to_previous(): lax.ppermute(value, 'blk', [(i, (i - 1) % count) for i in range(count)])]
  transfers between devices with their start and end apart: 15 -> 15, of which waited for: 3 -> 3; matrix products, arithmetic and copies ran while one was open for 0% -> 0% of each run, Pallas kernels for 32% -> 30%
where the time goes in v4:
time: 62.9 us; the launch traced here: 62.8 us
  starting transfers between devices  31.2 us (50%)
  Pallas kernels  20.3 us (32%)
  waiting for transfers between devices  9.11 us (14%)
  local copies, waits for them, and re-layouts  1.27 us (2%)
  between operations  1.01 us (2%)
    ppermute x9, starting transfers between devices, to_previous(): lax.ppermute(value, 'blk', [(i, (i - 1) % count) for i in range(count)])  30.7 us
    pallas_call x3, Pallas kernels, attend(): pl.pallas_call(functools.partial(attend_kernel, back, last), out_shape=ou...  10.4 us
    ppermute x6, waiting for transfers between devices, to_next(): lax.ppermute(value, 'blk', [(i, (i + 1) % count) for i in range(count)])  9.09 us
    pallas_call x1, Pallas kernels, mix(): pl.pallas_call(mix_kernel, out_shape=(jax.ShapeDtypeStruct(residual.shape...  3.61 us
    pallas_call x1, Pallas kernels, weigh(): pl.pallas_call(functools.partial(weigh_kernel, back), out_shape=(jax.Shap...  3.34 us
    pallas_call x1, Pallas kernels, down(): pl.pallas_call(functools.partial(down_kernel, slot), out_shape=jax.ShapeD...  1.63 us
    pallas_call x1, Pallas kernels, gate_up(): pl.pallas_call(functools.partial(gate_kernel, shards, slot), out_shape=ja...  1.29 us
    unnamed x18, local copies, waits for them, and re-layouts  1.27 us
  transfers between devices with their start and end apart: 15, of which 3 were waited for; matrix products, arithmetic and copies ran while one was open for 0% of the time, Pallas kernels for 30%

profile of v4, /device:TPU:0, one launch (start us, length us, event | category | flops | bytes accessed | tf_op | source)
XLA Modules:
  0.0 62.8 jit_solution(10533967066801170863)
XLA Ops:
  0.6 0.0 copy-start.6
  0.6 0.0 copy-start.7
  0.7 0.0 copy-start.2
  0.7 0.0 copy-start.3
  0.7 0.0 copy-start.8
  0.7 0.0 copy-start
  0.7 0.0 copy-start.5
  0.7 0.9 %copy-done.6 = bf16[256,1024]{1,0:T(8,128)(2,1)S(1)} copy-done((bf16[256,1024]{1,0:T(8,128)(2,1)S(1)}, bf16[256,1024]{1,0:T(8,128)(2,1)}, u32[]{:S(2)}) %copy-start.6) | copy-done | bytes 524312
  1.7 0.0 collective-permute-start.2
  1.7 0.2 copy-done.7
  1.8 0.0 collective-permute-start
  1.8 0.1 copy-done.2
  2.0 8.2 %collective-permute-start.6 = (bf16[56,4096]{1,0:T(8,128)(2,1)S(1)}, bf16[56,4096]{1,0:T(8,128)(2,1)S(1)}, u32[]{:S(2)}, u32[]{:S(2)}) collective-permute-start(bf16[56,4096]{1,0:T(8,128)(2,1)S(1)} %copy-done.2), channel_id=1, source_target_pairs={{0,255},{1,0},{2,1},{3,2},{4,3},{5,4},{6,5},{7,6},{8,7},{9,8},{10,... | collective-permute-start | bytes 1376264 | tf_op jit(solution)/shard_map/ppermute | solution.py:31
  10.2 0.0 copy-done.3
  10.2 0.7 %collective-permute-start.7 = (bf16[56,4096]{1,0:T(8,128)(2,1)S(1)}, bf16[56,4096]{1,0:T(8,128)(2,1)S(1)}, u32[]{:S(2)}, u32[]{:S(2)}) collective-permute-start(bf16[56,4096]{1,0:T(8,128)(2,1)S(1)} %copy-done.3), channel_id=1, source_target_pairs={{0,255},{1,0},{2,1},{3,2},{4,3},{5,4},{6,5},{7,6},{8,7},{9,8},{10,... | collective-permute-start | bytes 1376264 | tf_op jit(solution)/shard_map/ppermute | solution.py:31
  10.9 0.0 copy-done.8
  10.9 1.6 %collective-permute-start.12 = (bf16[56,4096]{1,0:T(8,128)(2,1)S(1)}, bf16[56,4096]{1,0:T(8,128)(2,1)S(1)}, u32[]{:S(2)}, u32[]{:S(2)}) collective-permute-start(bf16[56,4096]{1,0:T(8,128)(2,1)S(1)} %copy-done.8), channel_id=1, source_target_pairs={{0,255},{1,0},{2,1},{3,2},{4,3},{5,4},{6,5},{7,6},{8,7},{9,8},{10,... | collective-permute-start | bytes 1376264 | tf_op jit(solution)/shard_map/ppermute | solution.py:31
  12.5 0.0 copy-done
  12.5 0.0 copy-done.5
  12.5 3.2 %attend_0.1 = (f32[8,8,256]{2,1,0:T(8,128)S(1)}, f32[8,512,256]{2,1,0:T(8,128)S(1)}) custom-call(bf16[256,4096]{1,0:T(8,128)(2,1)S(1)} %copy-done, bf16[256,1024]{1,0:T(8,128)(2,1)S(1)} %copy-done.6, bf16[256,1024]{1,0:T(8,128)(2,1)S(1)} %copy-done.7, s32[1,256]{1,0:T(1,128)S(1)} %bitcast.3, f32[256,256]{1,0:T(8,128)S(1)} %causal.1.refs_4_), custom_call_target="tpu_custom_call" | custom-call | flops 1073741824 | bytes 12582912 | tf_op jit(solution)/shard_map/attend_0/pallas_call | solution.py:121
  15.7 1.1 %collective-permute-done.2.refs_1_ = bf16[256,1024]{1,0:T(8,128)(2,1)S(1)} collective-permute-done((bf16[256,1024]{1,0:T(8,128)(2,1)S(1)}, bf16[256,1024]{1,0:T(8,128)(2,1)S(1)}, u32[]{:S(2)}, u32[]{:S(2)}) %collective-permute-start.2) | collective-permute-done | bytes 524320 | tf_op jit(solution)/shard_map/ppermute | solution.py:26
  16.7 0.0 collective-permute-start.4
  16.7 5.6 %collective-permute-done.refs_2_ = bf16[256,1024]{1,0:T(8,128)(2,1)S(1)} collective-permute-done((bf16[256,1024]{1,0:T(8,128)(2,1)S(1)}, bf16[256,1024]{1,0:T(8,128)(2,1)S(1)}, u32[]{:S(2)}, u32[]{:S(2)}) %collective-permute-start) | collective-permute-done | bytes 524320 | tf_op jit(solution)/shard_map/ppermute | solution.py:26
  22.4 0.0 collective-permute-start.1
  22.4 0.0 collective-permute-done.6.refs_3_
  22.4 7.2 %collective-permute-start.8 = (bf16[56,4096]{1,0:T(8,128)(2,1)S(1)}, bf16[56,4096]{1,0:T(8,128)(2,1)S(1)}, u32[]{:S(2)}, u32[]{:S(2)}) collective-permute-start(bf16[56,4096]{1,0:T(8,128)(2,1)S(1)} %collective-permute-done.6.refs_3_), channel_id=1, source_target_pairs={{0,255},{1,0},{2,1},{3,2},{4,3},{5,4},{6,5},{7,6},{8,7},{9,8},{10,... | collective-permute-start | bytes 1376264 | tf_op jit(solution)/shard_map/ppermute | solution.py:31
  29.5 0.0 collective-permute-done.7.refs_4_
  29.5 0.3 collective-permute-start.9
  29.8 3.6 %attend_1.1 = (f32[8,8,256]{2,1,0:T(8,128)S(1)}, f32[8,512,256]{2,1,0:T(8,128)S(1)}) custom-call(bf16[256,4096]{1,0:T(8,128)(2,1)S(1)} %copy-done, bf16[256,1024]{1,0:T(8,128)(2,1)S(1)} %collective-permute-done.2.refs_1_, bf16[256,1024]{1,0:T(8,128)(2,1)S(1)} %collective-permute-done.refs_2_, s32[1,256]{1,0:T(1,128)S(1)} %bitcast.4, ...), custom_call_target="tpu_custom_call" | custom-call | flops 1073741824 | bytes 12582912 | tf_op jit(solution)/shard_map/attend_1/pallas_call | solution.py:121
  33.4 0.0 collective-permute-done.12.refs_2_
  33.4 0.1 collective-permute-start.13
  33.5 0.0 collective-permute-done.4.refs_1_
  33.5 0.5 collective-permute-start.5
  34.0 2.4 %collective-permute-done.1.refs_2_ = bf16[256,1024]{1,0:T(8,128)(2,1)S(1)} collective-permute-done((bf16[256,1024]{1,0:T(8,128)(2,1)S(1)}, bf16[256,1024]{1,0:T(8,128)(2,1)S(1)}, u32[]{:S(2)}, u32[]{:S(2)}) %collective-permute-start.1) | collective-permute-done | bytes 524320 | tf_op jit(solution)/shard_map/ppermute | solution.py:26
  36.4 0.0 collective-permute-start.3
  36.4 0.0 collective-permute-done.8.refs_5_
  36.4 7.2 %collective-permute-start.10 = (bf16[56,4096]{1,0:T(8,128)(2,1)S(1)}, bf16[56,4096]{1,0:T(8,128)(2,1)S(1)}, u32[]{:S(2)}, u32[]{:S(2)}) collective-permute-start(bf16[56,4096]{1,0:T(8,128)(2,1)S(1)} %collective-permute-done.8.refs_5_), channel_id=1, source_target_pairs={{0,255},{1,0},{2,1},{3,2},{4,3},{5,4},{6,5},{7,6},{8,7},{9,8},{10,... | collective-permute-start | bytes 1376264 | tf_op jit(solution)/shard_map/ppermute | solution.py:31
  43.6 3.6 %attend_2.1 = (f32[8,8,256]{2,1,0:T(8,128)S(1)}, f32[8,512,256]{2,1,0:T(8,128)S(1)}) custom-call(bf16[256,4096]{1,0:T(8,128)(2,1)S(1)} %copy-done, bf16[256,1024]{1,0:T(8,128)(2,1)S(1)} %collective-permute-done.4.refs_1_, bf16[256,1024]{1,0:T(8,128)(2,1)S(1)} %collective-permute-done.1.refs_2_, s32[1,256]{1,0:T(1,128)S(1)} %bitcast.5, ...), custom_call_target="tpu_custom_call" | custom-call | flops 1073741824 | bytes 12582912 | tf_op jit(solution)/shard_map/attend_2/pallas_call | solution.py:121
  47.2 0.0 copy-start.1
  47.2 0.0 copy-start.4
  47.2 0.0 collective-permute-done.9.refs_6_
  47.2 0.6 collective-permute-start.11
  47.8 0.0 collective-permute-done.13.refs_3_
  47.8 4.9 %collective-permute-start.14 = (bf16[56,4096]{1,0:T(8,128)(2,1)S(1)}, bf16[56,4096]{1,0:T(8,128)(2,1)S(1)}, u32[]{:S(2)}, u32[]{:S(2)}) collective-permute-start(bf16[56,4096]{1,0:T(8,128)(2,1)S(1)} %collective-permute-done.13.refs_3_), channel_id=1, source_target_pairs={{0,255},{1,0},{2,1},{3,2},{4,3},{5,4},{6,5},{7,6},{8,7},{9,8},{10,... | collective-permute-start | bytes 1376264 | tf_op jit(solution)/shard_map/ppermute | solution.py:31
  52.7 0.0 collective-permute-done.5.k_ref
  52.7 3.3 %weigh_3.1 = (bf16[8,1024,256]{2,1,0:T(8,128)(2,1)S(1)}, f32[8,8,256]{2,1,0:T(8,128)S(1)}) custom-call(bf16[256,4096]{1,0:T(8,128)(2,1)S(1)} %copy-done, bf16[256,1024]{1,0:T(8,128)(2,1)S(1)} %collective-permute-done.5.k_ref, s32[1,256]{1,0:T(1,128)S(1)} %bitcast.6, f32[8,8,256]{2,1,0:T(8,128)S(1)} %get-tuple-element.37.stat_ref), custom_call_target="tpu_custom_call" | custom-call | flops 536870912 | bytes 8388608 | tf_op jit(solution)/shard_map/weigh_3/pallas_call | solution.py:169
  56.0 0.0 collective-permute-done.3.v_ref
  56.1 0.0 copy-done.1
  56.1 0.0 copy-done.4
  56.1 3.6 %mix.1 = (bf16[256,4096]{1,0:T(8,128)(2,1)}, bf16[256,4096]{1,0:T(8,128)(2,1)S(1)}) custom-call(bf16[256,1024]{1,0:T(8,128)(2,1)S(1)} %collective-permute-done.3.v_ref, bf16[8,1024,256]{2,1,0:T(8,128)(2,1)S(1)} %get-tuple-element.38.weights_ref, f32[8,8,256]{2,1,0:T(8,128)S(1)} %get-tuple-element.39.stat_ref, f32[8,512,256]{2,1,0:T(8,128)S(1)} %get-tuple-element.40.sum_ref, ...), custom_call_target="tpu_custom_call" | custom-call | flops 536870912 | bytes 12582912 | tf_op jit(solution)/shard_map/mix/pallas_call | solution.py:219
  59.7 0.0 collective-permute-done.10.refs_7_
  59.7 0.0 collective-permute-done.11.refs_8_
  59.7 1.3 %gate_up_4.1.refs_0_ = bf16[256,256]{1,0:T(8,128)(2,1)S(1)} custom-call(bf16[256,4096]{1,0:T(8,128)(2,1)S(1)} %get-tuple-element.42.refs_0_, bf16[56,4096]{1,0:T(8,128)(2,1)S(1)} %copy-done.2, bf16[56,4096]{1,0:T(8,128)(2,1)S(1)} %copy-done.3, bf16[56,4096]{1,0:T(8,128)(2,1)S(1)} %collective-permute-done.6.refs_3_, ...), custom_call_target="tpu_custom_call" | custom-call | flops 939524096 | bytes 5767168 | tf_op jit(solution)/shard_map/gate_up_4/pallas_call | solution.py:304
  61.0 0.0 collective-permute-done.14.refs_4_
  61.0 1.6 %down.1 = bf16[256,4096]{1,0:T(8,128)(2,1)} custom-call(bf16[256,256]{1,0:T(8,128)(2,1)S(1)} %gate_up_4.1.refs_0_, bf16[56,4096]{1,0:T(8,128)(2,1)S(1)} %copy-done.8, bf16[56,4096]{1,0:T(8,128)(2,1)S(1)} %collective-permute-done.12.refs_2_, bf16[56,4096]{1,0:T(8,128)(2,1)S(1)} %collective-permute-done.13.refs_3_, ...), custom_call_target="tpu_custom_call" | custom-call | flops 30064771072 | bytes 4194304 | tf_op jit(solution)/shard_map/down/pallas_call | solution.py:322
  (1 shorter events, 0.0 us)
Async XLA Ops:
  0.6 1.0 %copy-start.6 = (bf16[256,1024]{1,0:T(8,128)(2,1)S(1)}, bf16[256,1024]{1,0:T(8,128)(2,1)}, u32[]{:S(2)}) copy-start(bf16[256,1024]{1,0:T(8,128)(2,1)} %refs_1_.3) | copy-start | bytes 1572868
  0.6 1.2 %copy-start.7 = (bf16[256,1024]{1,0:T(8,128)(2,1)S(1)}, bf16[256,1024]{1,0:T(8,128)(2,1)}, u32[]{:S(2)}) copy-start(bf16[256,1024]{1,0:T(8,128)(2,1)} %refs_2_.2) | copy-start | bytes 1572868
  0.7 1.3 %copy-start.2 = (bf16[56,4096]{1,0:T(8,128)(2,1)S(1)}, bf16[56,4096]{1,0:T(8,128)(2,1)}, u32[]{:S(2)}) copy-start(bf16[56,4096]{1,0:T(8,128)(2,1)} %refs_1_.4) | copy-start | bytes 1376260
  0.7 9.5 %copy-start.3 = (bf16[56,4096]{1,0:T(8,128)(2,1)S(1)}, bf16[56,4096]{1,0:T(8,128)(2,1)}, u32[]{:S(2)}) copy-start(bf16[56,4096]{1,0:T(8,128)(2,1)} %refs_2_.3) | copy-start | bytes 1376260
  0.7 10.2 %copy-start.8 = (bf16[56,4096]{1,0:T(8,128)(2,1)S(1)}, bf16[56,4096]{1,0:T(8,128)(2,1)}, u32[]{:S(2)}) copy-start(bf16[56,4096]{1,0:T(8,128)(2,1)} %refs_1_.5) | copy-start | bytes 1376260
  0.7 11.8 %copy-start = (bf16[256,4096]{1,0:T(8,128)(2,1)S(1)}, bf16[256,4096]{1,0:T(8,128)(2,1)}, u32[]{:S(2)}) copy-start(bf16[256,4096]{1,0:T(8,128)(2,1)} %q_ref.1) | copy-start | bytes 6291460
  0.7 11.8 %copy-start.5 = (s32[256]{0:T(256)S(1)}, s32[256]{0:T(256)}, u32[]{:S(2)}) copy-start(s32[256]{0:T(256)} %param.12) | copy-start | bytes 3076
  1.7 15.1 %collective-permute-start.2 = (bf16[256,1024]{1,0:T(8,128)(2,1)S(1)}, bf16[256,1024]{1,0:T(8,128)(2,1)S(1)}, u32[]{:S(2)}, u32[]{:S(2)}) collective-permute-start(bf16[256,1024]{1,0:T(8,128)(2,1)S(1)} %copy-done.6), channel_id=1, source_target_pairs={{0,1},{1,2},{2,3},{3,4},{4,5},{5,6},{6,7},{7,8},{8,9},{9,10},{10,1... | collective-permute-start | bytes 1572872 | tf_op jit(solution)/shard_map/ppermute | solution.py:26
  1.8 20.5 %collective-permute-start = (bf16[256,1024]{1,0:T(8,128)(2,1)S(1)}, bf16[256,1024]{1,0:T(8,128)(2,1)S(1)}, u32[]{:S(2)}, u32[]{:S(2)}) collective-permute-start(bf16[256,1024]{1,0:T(8,128)(2,1)S(1)} %copy-done.7), channel_id=1, source_target_pairs={{0,1},{1,2},{2,3},{3,4},{4,5},{5,6},{6,7},{7,8},{8,9},{9,10},{10,1... | collective-permute-start | bytes 1572872 | tf_op jit(solution)/shard_map/ppermute | solution.py:26
  2.0 20.4 %collective-permute-start.6 = (bf16[56,4096]{1,0:T(8,128)(2,1)S(1)}, bf16[56,4096]{1,0:T(8,128)(2,1)S(1)}, u32[]{:S(2)}, u32[]{:S(2)}) collective-permute-start(bf16[56,4096]{1,0:T(8,128)(2,1)S(1)} %copy-done.2), channel_id=1, source_target_pairs={{0,255},{1,0},{2,1},{3,2},{4,3},{5,4},{6,5},{7,6},{8,7},{9,8},{10,... | collective-permute-start | bytes 1376264 | tf_op jit(solution)/shard_map/ppermute | solution.py:31
  10.2 19.4 %collective-permute-start.7 = (bf16[56,4096]{1,0:T(8,128)(2,1)S(1)}, bf16[56,4096]{1,0:T(8,128)(2,1)S(1)}, u32[]{:S(2)}, u32[]{:S(2)}) collective-permute-start(bf16[56,4096]{1,0:T(8,128)(2,1)S(1)} %copy-done.3), channel_id=1, source_target_pairs={{0,255},{1,0},{2,1},{3,2},{4,3},{5,4},{6,5},{7,6},{8,7},{9,8},{10,... | collective-permute-start | bytes 1376264 | tf_op jit(solution)/shard_map/ppermute | solution.py:31
  10.9 22.6 %collective-permute-start.12 = (bf16[56,4096]{1,0:T(8,128)(2,1)S(1)}, bf16[56,4096]{1,0:T(8,128)(2,1)S(1)}, u32[]{:S(2)}, u32[]{:S(2)}) collective-permute-start(bf16[56,4096]{1,0:T(8,128)(2,1)S(1)} %copy-done.8), channel_id=1, source_target_pairs={{0,255},{1,0},{2,1},{3,2},{4,3},{5,4},{6,5},{7,6},{8,7},{9,8},{10,... | collective-permute-start | bytes 1376264 | tf_op jit(solution)/shard_map/ppermute | solution.py:31
  16.7 16.8 %collective-permute-start.4 = (bf16[256,1024]{1,0:T(8,128)(2,1)S(1)}, bf16[256,1024]{1,0:T(8,128)(2,1)S(1)}, u32[]{:S(2)}, u32[]{:S(2)}) collective-permute-start(bf16[256,1024]{1,0:T(8,128)(2,1)S(1)} %collective-permute-done.2.refs_1_), channel_id=1, source_target_pairs={{0,1},{1,2},{2,3},{3,4},{4,5},{5,6},{6,7},{7,8},{8,9},{9,10},{10,1... | collective-permute-start | bytes 1572872 | tf_op jit(solution)/shard_map/ppermute | solution.py:26
  22.4 14.0 %collective-permute-start.1 = (bf16[256,1024]{1,0:T(8,128)(2,1)S(1)}, bf16[256,1024]{1,0:T(8,128)(2,1)S(1)}, u32[]{:S(2)}, u32[]{:S(2)}) collective-permute-start(bf16[256,1024]{1,0:T(8,128)(2,1)S(1)} %collective-permute-done.refs_2_), channel_id=1, source_target_pairs={{0,1},{1,2},{2,3},{3,4},{4,5},{5,6},{6,7},{7,8},{8,9},{9,10},{10,1... | collective-permute-start | bytes 1572872 | tf_op jit(solution)/shard_map/ppermute | solution.py:26
  22.4 14.0 %collective-permute-start.8 = (bf16[56,4096]{1,0:T(8,128)(2,1)S(1)}, bf16[56,4096]{1,0:T(8,128)(2,1)S(1)}, u32[]{:S(2)}, u32[]{:S(2)}) collective-permute-start(bf16[56,4096]{1,0:T(8,128)(2,1)S(1)} %collective-permute-done.6.refs_3_), channel_id=1, source_target_pairs={{0,255},{1,0},{2,1},{3,2},{4,3},{5,4},{6,5},{7,6},{8,7},{9,8},{10,... | collective-permute-start | bytes 1376264 | tf_op jit(solution)/shard_map/ppermute | solution.py:31
  29.5 17.7 %collective-permute-start.9 = (bf16[56,4096]{1,0:T(8,128)(2,1)S(1)}, bf16[56,4096]{1,0:T(8,128)(2,1)S(1)}, u32[]{:S(2)}, u32[]{:S(2)}) collective-permute-start(bf16[56,4096]{1,0:T(8,128)(2,1)S(1)} %collective-permute-done.7.refs_4_), channel_id=1, source_target_pairs={{0,255},{1,0},{2,1},{3,2},{4,3},{5,4},{6,5},{7,6},{8,7},{9,8},{10,... | collective-permute-start | bytes 1376264 | tf_op jit(solution)/shard_map/ppermute | solution.py:31
  33.4 14.4 %collective-permute-start.13 = (bf16[56,4096]{1,0:T(8,128)(2,1)S(1)}, bf16[56,4096]{1,0:T(8,128)(2,1)S(1)}, u32[]{:S(2)}, u32[]{:S(2)}) collective-permute-start(bf16[56,4096]{1,0:T(8,128)(2,1)S(1)} %collective-permute-done.12.refs_2_), channel_id=1, source_target_pairs={{0,255},{1,0},{2,1},{3,2},{4,3},{5,4},{6,5},{7,6},{8,7},{9,8},{10,... | collective-permute-start | bytes 1376264 | tf_op jit(solution)/shard_map/ppermute | solution.py:31
  33.5 19.2 %collective-permute-start.5 = (bf16[256,1024]{1,0:T(8,128)(2,1)S(1)}, bf16[256,1024]{1,0:T(8,128)(2,1)S(1)}, u32[]{:S(2)}, u32[]{:S(2)}) collective-permute-start(bf16[256,1024]{1,0:T(8,128)(2,1)S(1)} %collective-permute-done.4.refs_1_), channel_id=1, source_target_pairs={{0,1},{1,2},{2,3},{3,4},{4,5},{5,6},{6,7},{7,8},{8,9},{9,10},{10,1... | collective-permute-start | bytes 1572872 | tf_op jit(solution)/shard_map/ppermute | solution.py:26
  36.4 19.7 %collective-permute-start.3 = (bf16[256,1024]{1,0:T(8,128)(2,1)S(1)}, bf16[256,1024]{1,0:T(8,128)(2,1)S(1)}, u32[]{:S(2)}, u32[]{:S(2)}) collective-permute-start(bf16[256,1024]{1,0:T(8,128)(2,1)S(1)} %collective-permute-done.1.refs_2_), channel_id=1, source_target_pairs={{0,1},{1,2},{2,3},{3,4},{4,5},{5,6},{6,7},{7,8},{8,9},{9,10},{10,1... | collective-permute-start | bytes 1572872 | tf_op jit(solution)/shard_map/ppermute | solution.py:26
  36.4 23.3 %collective-permute-start.10 = (bf16[56,4096]{1,0:T(8,128)(2,1)S(1)}, bf16[56,4096]{1,0:T(8,128)(2,1)S(1)}, u32[]{:S(2)}, u32[]{:S(2)}) collective-permute-start(bf16[56,4096]{1,0:T(8,128)(2,1)S(1)} %collective-permute-done.8.refs_5_), channel_id=1, source_target_pairs={{0,255},{1,0},{2,1},{3,2},{4,3},{5,4},{6,5},{7,6},{8,7},{9,8},{10,... | collective-permute-start | bytes 1376264 | tf_op jit(solution)/shard_map/ppermute | solution.py:31
  47.2 8.9 %copy-start.1 = (bf16[256,4096]{1,0:T(8,128)(2,1)S(1)}, bf16[256,4096]{1,0:T(8,128)(2,1)}, u32[]{:S(2)}) copy-start(bf16[256,4096]{1,0:T(8,128)(2,1)} %residual_ref.1) | copy-start | bytes 6291460
  47.2 8.9 %copy-start.4 = (f32[4096]{0:T(1024)S(1)}, f32[4096]{0:T(1024)}, u32[]{:S(2)}) copy-start(f32[4096]{0:T(1024)} %param.14) | copy-start | bytes 49156
  47.2 12.5 %collective-permute-start.11 = (bf16[56,4096]{1,0:T(8,128)(2,1)S(1)}, bf16[56,4096]{1,0:T(8,128)(2,1)S(1)}, u32[]{:S(2)}, u32[]{:S(2)}) collective-permute-start(bf16[56,4096]{1,0:T(8,128)(2,1)S(1)} %collective-permute-done.9.refs_6_), channel_id=1, source_target_pairs={{0,255},{1,0},{2,1},{3,2},{4,3},{5,4},{6,5},{7,6},{8,7},{9,8},{10,... | collective-permute-start | bytes 1376264 | tf_op jit(solution)/shard_map/ppermute | solution.py:31
  47.8 13.2 %collective-permute-start.14 = (bf16[56,4096]{1,0:T(8,128)(2,1)S(1)}, bf16[56,4096]{1,0:T(8,128)(2,1)S(1)}, u32[]{:S(2)}, u32[]{:S(2)}) collective-permute-start(bf16[56,4096]{1,0:T(8,128)(2,1)S(1)} %collective-permute-done.13.refs_3_), channel_id=1, source_target_pairs={{0,255},{1,0},{2,1},{3,2},{4,3},{5,4},{6,5},{7,6},{8,7},{9,8},{10,... | collective-permute-start | bytes 1376264 | tf_op jit(solution)/shard_map/ppermute | solution.py:31
